TPU v7x, 256 devices: a whole 4x4x8 slice. The times are simulated.
256 devices in a mesh: seq: 32 (over y_lo, z, core), tp: 8 (over x, y_hi).
Axes of the slice: x: 4, y: 4 (y_hi: 2, y_lo: 2; y = y_hi * 2 + y_lo), z: 8, core: 2. Of those that a mesh axis runs over, the one named last changes fastest.
Arguments:
- query: bfloat16 [6144, 5120], P('seq', 'tp')
- span_keys: bfloat16 [6144, 5120], P('seq', 'tp'), may hold values from -6 to 6
- span_values: bfloat16 [6144, 5120], P('seq', 'tp'), may hold values from -48 to 48
- cache_keys: bfloat16 [8, 8192, 5120], P(None, 'seq', 'tp'), may hold values from -6 to 6
- cache_values: bfloat16 [8, 8192, 5120], P(None, 'seq', 'tp'), may hold values from -48 to 48
- out_weight: bfloat16 [5120, 5120], P('tp'), may hold values from -0.078125 to 0.078125
- cache_lengths: int32 [8], replicated, may hold values from 1 to 8192, as said below
- sink_counts: int32 [8], replicated, may hold values from 1 to 256, as said below
- windows: int32 [8], replicated, may hold values from 2048 to 4096, as said below
- block_of_slot: int32 [8, 32], replicated, may hold values from 0 to 31, each once within a row
Outputs:
- projected: bfloat16 [6144, 5120], P('seq', 'tp')
Inputs may be any that keep to these rules, and one draw needn't show every extreme that they name: `cache_lengths`: at least 1 and at most 8192; some request has exactly 8192. `sink_counts`: some request has exactly 256. `windows`: some request has exactly 4096. `block_of_slot`: each row is a permutation of 0 to 31.
All inputs are finite; a program needn't handle non-finite values.
Results may differ from a plain program's by a relative error of at most 0.015.
Values may be sent and summed in bfloat16 or wider, within the bound.
A program may use at most 192 MiB of HBM per device.

v0:
```python
import math

import jax
import jax.numpy as jnp
from jax import lax
from jax.sharding import PartitionSpec as P

HEAD = 128
GROUP = 4


NEG = -1e30


def shifted(value, axis, steps):
    count = lax.axis_size(axis)
    initial, last = (max(0, -steps), min(count, count - steps))
    return lax.ppermute(value, axis, [(source, source + steps) for source in range(initial, last)])


def visible(query_pos, key_pos, valid, window, sinks):
    later = query_pos[:, None]
    earlier = key_pos[None, :]
    near = later - earlier < window
    return (earlier <= later) & (near | (earlier < sinks)) & valid[None, :]


def block_partial(q_rows, keys, vals, query_pos, key_pos, valid, window, sinks):
    mask = visible(query_pos, key_pos, valid, window, sinks)
    scale = 1.0 / math.sqrt(q_rows.shape[-1])
    scores = jnp.einsum("qhd,khd->hqk", q_rows, keys, preferred_element_type=jnp.float32) * scale
    scores = jnp.where(mask[None], scores, NEG)
    top = jnp.max(scores, axis=2)
    weights = jnp.where(mask[None], jnp.exp(scores - top[:, :, None]), 0.0)
    total = jnp.sum(weights, axis=2)
    summed = jnp.einsum(
        "hqk,khd->qhd", weights.astype(jnp.bfloat16), vals, preferred_element_type=jnp.float32
    )
    return (summed, top.T, total.T)


def merge_partial(first, second):
    top = jnp.maximum(first[1], second[1])
    scale_a = jnp.exp(first[1] - top)
    scale_b = jnp.exp(second[1] - top)
    summed = first[0] * scale_a[..., None] + second[0] * scale_b[..., None]
    return (summed, top, first[2] * scale_a + second[2] * scale_b)


def shards(
    query,
    span_keys,
    span_values,
    cache_keys,
    cache_values,
    out_weight,
    cache_lengths,
    sink_counts,
    windows,
    block_of_slot,
):
    rows, width = query.shape
    heads_here = width // HEAD
    devices = lax.axis_size("seq")
    me = lax.axis_index("seq")
    requests = cache_keys.shape[0]
    mine = me % requests
    place = me // requests
    cache_dev = cache_keys.shape[1]
    length = cache_lengths[mine]
    window = windows[mine]
    sinks = sink_counts[mine]
    own_pos = length + place * rows + jnp.arange(rows, dtype=jnp.int32)
    all_valid = jnp.ones((rows,), jnp.bool_)
    spread_keys = jnp.tile(cache_keys, (GROUP, 1, 1))
    spread_vals = jnp.tile(cache_values, (GROUP, 1, 1))
    got_keys, got_vals = (
        lax.all_to_all(spread_keys, "seq", split_axis=0, concat_axis=0, tiled=True),
        lax.all_to_all(spread_vals, "seq", split_axis=0, concat_axis=0, tiled=True),
    )
    q_rows = query.reshape(rows, heads_here, HEAD)
    slot_pos = (
        block_of_slot[mine][:, None] * cache_dev + jnp.arange(cache_dev, dtype=jnp.int32)[None, :]
    )
    per_block = max(1, min(devices, 1024 // cache_dev))
    blocks = devices // per_block
    key_blocks = got_keys.reshape(blocks, per_block * cache_dev, heads_here, HEAD)
    val_blocks = got_vals.reshape(blocks, per_block * cache_dev, heads_here, HEAD)
    pos_blocks = slot_pos.reshape(blocks, per_block * cache_dev)

    def step_block(carry, inputs):
        keys, vals, key_pos = inputs
        part_now = block_partial(
            q_rows, keys, vals, own_pos, key_pos, key_pos < length, window, sinks
        )
        return (merge_partial(carry, part_now), None)

    start = (
        jnp.zeros((rows, heads_here, HEAD), jnp.float32),
        jnp.full((rows, heads_here), NEG, jnp.float32),
        jnp.zeros((rows, heads_here), jnp.float32),
    )
    carry, unused = lax.scan(step_block, start, (key_blocks, val_blocks, pos_blocks))
    carry = merge_partial(
        carry,
        block_partial(
            q_rows,
            span_keys.reshape(rows, heads_here, HEAD),
            span_values.reshape(rows, heads_here, HEAD),
            own_pos,
            own_pos,
            all_valid,
            window,
            sinks,
        ),
    )
    for back in range(1, GROUP):
        prior_keys, prior_vals = shifted((span_keys, span_values), "seq", back * requests)
        prior_pos = length + (place - back) * rows + jnp.arange(rows, dtype=jnp.int32)
        prior_valid = jnp.broadcast_to(place >= back, (rows,))
        carry = merge_partial(
            carry,
            block_partial(
                q_rows,
                prior_keys.reshape(rows, heads_here, HEAD),
                prior_vals.reshape(rows, heads_here, HEAD),
                own_pos,
                prior_pos,
                prior_valid,
                window,
                sinks,
            ),
        )
    summed, top, total = carry
    attention = (summed / total[..., None]).astype(jnp.bfloat16).reshape(rows, width)
    terms = jnp.dot(attention, out_weight, preferred_element_type=jnp.float32)
    return lax.psum_scatter(terms.astype(jnp.bfloat16), "tp", scatter_dimension=1, tiled=True)


def solution(mesh):
    return jax.shard_map(
        shards,
        mesh=mesh,
        in_specs=(
            P("seq", "tp"),
            P("seq", "tp"),
            P("seq", "tp"),
            P(None, "seq", "tp"),
            P(None, "seq", "tp"),
            P("tp", None),
            P(),
            P(),
            P(),
            P(),
        ),
        out_specs=P("seq", "tp"),
        check_vma=False,
    )
```

profile of v0, /device:TPU:224, one launch (start us, length us, event | category | flops | bytes accessed | tf_op | source)
XLA Modules:
  0.0 850.2 jit_solution(205975982290722817)
XLA Ops:
  6.5 3.0 copy.51
  9.5 5.2 tile.8
  14.7 7.1 all-to-all-start
  21.7 3.0 copy.54
  24.7 227.3 %all-to-all-done = bf16[32,256,640]{1,2,0:T(8,128)(2,1)} async-done(((bf16[32,256,640]{1,2,0:T(8,128)(2,1)}), bf16[32,256,640]{1,2,0:T(8,128)(2,1)}, u32[]{:S(2)}, u32[]{:S(2)}) %all-to-all-start) | async-done | bytes 10485792 | tf_op jit(solution)/shard_map/all_to_all | solution.py:78
  252.0 5.0 tile.20
  257.1 9.6 %all-to-all-start.1 = ((bf16[32,256,640]{1,2,0:T(8,128)(2,1)}), bf16[32,256,640]{1,2,0:T(8,128)(2,1)}, u32[]{:S(2)}, u32[]{:S(2)}) async-start(bf16[32,256,640]{1,2,0:T(8,128)(2,1)} %bitcast.213), calls=%async_computation.1 | async-start | bytes 20971520 | tf_op jit(solution)/shard_map/all_to_all | solution.py:79
  266.8 6.1 collective-permute-start
  272.9 2.0 collective-permute-start.2
  276.3 2.0 collective-permute-start.3
  288.5 219.6 %collective-permute-done = bf16[192,640]{1,0:T(8,128)(2,1)S(1)} collective-permute-done((bf16[192,640]{1,0:T(8,128)(2,1)S(1)}, bf16[192,640]{1,0:T(8,128)(2,1)S(1)}, u32[]{:S(2)}, u32[]{:S(2)}) %collective-permute-start) | collective-permute-done | bytes 245792 | tf_op jit(solution)/shard_map/ppermute | solution.py:18
  508.2 9.1 %collective-permute-start.1 = (bf16[192,640]{1,0:T(8,128)(2,1)S(1)}, bf16[192,640]{1,0:T(8,128)(2,1)S(1)}, u32[]{:S(2)}, u32[]{:S(2)}) collective-permute-start(bf16[192,640]{1,0:T(8,128)(2,1)S(1)} %copy-done.16), channel_id=1, source_target_pairs={{0,64},{8,72},{16,80},{24,88},{32,96},{40,104},{48,112},{56,120},{... | collective-permute-start | bytes 737288 | tf_op jit(solution)/shard_map/ppermute | solution.py:18
  535.5 13.8 %copy.52 = bf16[32,256,640]{1,0,2:T(8,128)(2,1)} copy(bf16[32,256,640]{1,2,0:T(8,128)(2,1)} %all-to-all-done) | data formatting | bytes 20971520 | tf_op jit(solution)/shard_map/all_to_all | solution.py:78
  549.3 17.1 %reshape.487 = bf16[8,1024,5,128]{1,0,3,2:T(8,128)(2,1)} reshape(bf16[32,256,640]{1,0,2:T(8,128)(2,1)} %copy.52) | data formatting | bytes 20971520 | tf_op jit(solution)/shard_map/reshape | solution.py:87
  566.4 15.1 %copy.56 = bf16[8,1024,5,128]{3,1,2,0:T(8,128)(2,1)} copy(bf16[8,1024,5,128]{1,0,3,2:T(8,128)(2,1)} %reshape.487) | data formatting | bytes 20971520
  581.4 13.8 %copy.55 = bf16[32,256,640]{1,0,2:T(8,128)(2,1)} copy(bf16[32,256,640]{1,2,0:T(8,128)(2,1)} %all-to-all-done.1) | data formatting | bytes 20971520 | tf_op jit(solution)/shard_map/all_to_all | solution.py:79
  595.2 17.1 %reshape.489 = bf16[8,1024,5,128]{1,0,3,2:T(8,128)(2,1)} reshape(bf16[32,256,640]{1,0,2:T(8,128)(2,1)} %copy.55) | data formatting | bytes 20971520 | tf_op jit(solution)/shard_map/reshape | solution.py:88
  612.3 15.1 %copy.58 = bf16[8,1024,5,128]{3,1,2,0:T(8,128)(2,1)} copy(bf16[8,1024,5,128]{1,0,3,2:T(8,128)(2,1)} %reshape.489) | data formatting | bytes 20971520
  627.4 106.5 %while.15 = (s32[]{:T(128)}, f32[192,5,128]{2,0,1:T(8,128)}, f32[192,5]{0,1:T(8,128)S(1)}, f32[192,5]{0,1:T(8,128)S(1)}, s32[8,1024]{1,0:T(8,128)}, /*index=5*/s...) while((s32[]{:T(128)}, f32[192,5,128]{2,0,1:T(8,128)}, ...), condition=%wide.region_3.4_spmd.clone, body=%wide.region_0.3_spmd.clone.sunk | while | flops 517775168 | bytes 32234684 | solution.py:103
  627.4 2.0 compare_reduce_fusion.3
  630.4 2.2 fusion.143
  636.0 4.6 fusion.146
  640.6 2.0 compare_reduce_fusion.3
  643.7 2.2 fusion.143
  645.9 2.0 copy-done
  649.2 4.7 fusion.146
  653.9 2.0 compare_reduce_fusion.3
  657.0 2.2 fusion.143
  662.6 4.7 fusion.146
  667.2 2.0 compare_reduce_fusion.3
  670.3 2.2 fusion.143
  675.9 4.7 fusion.146
  680.6 2.0 compare_reduce_fusion.3
  683.6 2.2 fusion.143
  685.9 2.0 copy-done
  689.2 4.7 fusion.146
  693.9 2.0 compare_reduce_fusion.3
  696.9 2.2 fusion.143
  702.5 4.7 fusion.146
  707.2 2.0 compare_reduce_fusion.3
  710.3 2.2 fusion.143
  715.8 4.7 fusion.146
  720.5 2.0 compare_reduce_fusion.3
  723.6 2.2 fusion.143
  729.2 4.7 fusion.146
  739.6 4.6 convolution_convert_fusion
  744.2 2.5 copy.100
  746.8 94.8 %reduce-scatter.4.cloned.1.call-done = bf16[640,192]{1,0:T(8,128)(2,1)} async-done(((bf16[5120,192]{1,0:T(8,128)(2,1)}), bf16[640,192]{1,0:T(8,128)(2,1)}) %reduce-scatter.4.cloned.1.call-update) | async-done | bytes 245776
  (143 shorter events, 65.3 us)
Async XLA Ops:
  14.7 237.4 %all-to-all-start = ((bf16[32,256,640]{1,2,0:T(8,128)(2,1)}), bf16[32,256,640]{1,2,0:T(8,128)(2,1)}, u32[]{:S(2)}, u32[]{:S(2)}) async-start(bf16[32,256,640]{1,2,0:T(8,128)(2,1)} %bitcast.214), calls=%async_computation | async-start | bytes 20971520 | tf_op jit(solution)/shard_map/all_to_all | solution.py:78
  257.0 9.7 %copy-start.15 = (bf16[192,640]{1,0:T(8,128)(2,1)S(1)}, bf16[192,640]{1,0:T(8,128)(2,1)}, u32[]{:S(2)}) copy-start(bf16[192,640]{1,0:T(8,128)(2,1)} %param.13) | copy-start | bytes 737284
  257.0 19.2 %copy-start.16 = (bf16[192,640]{1,0:T(8,128)(2,1)S(1)}, bf16[192,640]{1,0:T(8,128)(2,1)}, u32[]{:S(2)}) copy-start(bf16[192,640]{1,0:T(8,128)(2,1)} %param.14) | copy-start | bytes 737284
  257.0 22.8 %copy-start.20 = (s32[8]{0:T(128)S(1)}, s32[8]{0:T(128)}, u32[]{:S(2)}) copy-start(s32[8]{0:T(128)} %param.18) | copy-start | bytes 100
  257.0 23.4 %copy-start.21 = (s32[8]{0:T(128)S(1)}, s32[8]{0:T(128)}, u32[]{:S(2)}) copy-start(s32[8]{0:T(128)} %param.20) | copy-start | bytes 100
  257.0 24.1 %copy-start.22 = (s32[8]{0:T(128)S(1)}, s32[8]{0:T(128)}, u32[]{:S(2)}) copy-start(s32[8]{0:T(128)} %param.19) | copy-start | bytes 100
  257.1 24.7 %copy-start.14 = (bf16[192,640]{1,0:T(8,128)(2,1)S(1)}, bf16[192,640]{1,0:T(8,128)(2,1)}, u32[]{:S(2)}) copy-start(bf16[192,640]{1,0:T(8,128)(2,1)} %param.12) | copy-start | bytes 737284
  257.1 324.4 %all-to-all-start.1 = ((bf16[32,256,640]{1,2,0:T(8,128)(2,1)}), bf16[32,256,640]{1,2,0:T(8,128)(2,1)}, u32[]{:S(2)}, u32[]{:S(2)}) async-start(bf16[32,256,640]{1,2,0:T(8,128)(2,1)} %bitcast.213), calls=%async_computation.1 | async-start | bytes 20971520 | tf_op jit(solution)/shard_map/all_to_all | solution.py:79
  266.7 574.9 %reduce-scatter.4.cloned.1.call-start = ((), (), s32[]{:S(2)}) async-start(), calls=%async_computation.3 | async-start | bytes 2949120
  266.8 241.4 %collective-permute-start = (bf16[192,640]{1,0:T(8,128)(2,1)S(1)}, bf16[192,640]{1,0:T(8,128)(2,1)S(1)}, u32[]{:S(2)}, u32[]{:S(2)}) collective-permute-start(bf16[192,640]{1,0:T(8,128)(2,1)S(1)} %copy-done.15), channel_id=1, source_target_pairs={{0,64},{8,72},{16,80},{24,88},{32,96},{40,104},{48,112},{56,120},{... | collective-permute-start | bytes 737288 | tf_op jit(solution)/shard_map/ppermute | solution.py:18
  272.9 247.3 %collective-permute-start.2 = (bf16[192,640]{1,0:T(8,128)(2,1)S(1)}, bf16[192,640]{1,0:T(8,128)(2,1)}, u32[]{:S(2)}, u32[]{:S(2)}) collective-permute-start(bf16[192,640]{1,0:T(8,128)(2,1)S(1)} %copy-done.15), channel_id=1, source_target_pairs={{0,128},{8,136},{16,144},{24,152},{32,160},{40,168},{48,176},{56,1... | collective-permute-start | bytes 737288 | tf_op jit(solution)/shard_map/ppermute | solution.py:18
  274.9 246.4 %collective-permute-start.4 = (bf16[192,640]{1,0:T(8,128)(2,1)S(1)}, bf16[192,640]{1,0:T(8,128)(2,1)}, u32[]{:S(2)}, u32[]{:S(2)}) collective-permute-start(bf16[192,640]{1,0:T(8,128)(2,1)S(1)} %copy-done.15), channel_id=1, source_target_pairs={{0,192},{8,200},{16,208},{24,216},{32,224},{40,232},{48,240},{56,2... | collective-permute-start | bytes 737288 | tf_op jit(solution)/shard_map/ppermute | solution.py:18
  276.3 246.9 %collective-permute-start.3 = (bf16[192,640]{1,0:T(8,128)(2,1)S(1)}, bf16[192,640]{1,0:T(8,128)(2,1)}, u32[]{:S(2)}, u32[]{:S(2)}) collective-permute-start(bf16[192,640]{1,0:T(8,128)(2,1)S(1)} %copy-done.16), channel_id=1, source_target_pairs={{0,128},{8,136},{16,144},{24,152},{32,160},{40,168},{48,176},{56,1... | collective-permute-start | bytes 737288 | tf_op jit(solution)/shard_map/ppermute | solution.py:18
  278.3 246.8 %collective-permute-start.5 = (bf16[192,640]{1,0:T(8,128)(2,1)S(1)}, bf16[192,640]{1,0:T(8,128)(2,1)}, u32[]{:S(2)}, u32[]{:S(2)}) collective-permute-start(bf16[192,640]{1,0:T(8,128)(2,1)S(1)} %copy-done.16), channel_id=1, source_target_pairs={{0,192},{8,200},{16,208},{24,216},{32,224},{40,232},{48,240},{56,2... | collective-permute-start | bytes 737288 | tf_op jit(solution)/shard_map/ppermute | solution.py:18
  287.3 229.9 %copy-start.5 = (pred[192,192]{0,1:T(8,128)(4,1)}, pred[192,192]{0,1:T(8,128)(4,1)S(1)}, u32[]{:S(2)}) copy-start(pred[192,192]{0,1:T(8,128)(4,1)S(1)} %get-tuple-element.180) | copy-start | bytes 110596
  287.3 242.7 %copy-start.11 = (pred[192,192]{0,1:T(8,128)(4,1)}, pred[192,192]{0,1:T(8,128)(4,1)S(1)}, u32[]{:S(2)}) copy-start(pred[192,192]{0,1:T(8,128)(4,1)S(1)} %get-tuple-element.181) | copy-start | bytes 110596
  287.4 244.0 %copy-start.8 = (pred[192,192]{0,1:T(8,128)(4,1)}, pred[192,192]{0,1:T(8,128)(4,1)S(1)}, u32[]{:S(2)}) copy-start(pred[192,192]{0,1:T(8,128)(4,1)S(1)} %get-tuple-element.182) | copy-start | bytes 110596
  508.2 20.6 %collective-permute-start.1 = (bf16[192,640]{1,0:T(8,128)(2,1)S(1)}, bf16[192,640]{1,0:T(8,128)(2,1)S(1)}, u32[]{:S(2)}, u32[]{:S(2)}) collective-permute-start(bf16[192,640]{1,0:T(8,128)(2,1)S(1)} %copy-done.16), channel_id=1, source_target_pairs={{0,64},{8,72},{16,80},{24,88},{32,96},{40,104},{48,112},{56,120},{... | collective-permute-start | bytes 737288 | tf_op jit(solution)/shard_map/ppermute | solution.py:18
  529.7 2.5 copy-start.4
  530.0 1.0 copy-start.1
  530.0 2.1 copy-start.18
  533.3 0.6 copy-start.17
  627.4 107.4 %copy-start.9 = (pred[192,192]{0,1:T(8,128)(4,1)S(1)}, pred[192,192]{0,1:T(8,128)(4,1)}, u32[]{:S(2)}) copy-start(pred[192,192]{0,1:T(8,128)(4,1)} %copy-done.8) | copy-start | bytes 110596
  627.4 108.9 %copy-start.7 = (pred[192,192]{0,1:T(8,128)(4,1)S(1)}, pred[192,192]{0,1:T(8,128)(4,1)}, u32[]{:S(2)}) copy-start(pred[192,192]{0,1:T(8,128)(4,1)} %get-tuple-element.183) | copy-start | bytes 110596
  632.7 2.0 copy-start
  645.9 2.0 copy-start
  659.2 2.0 copy-start
  672.5 2.0 copy-start
  685.9 2.0 copy-start
  699.2 2.0 copy-start
  712.5 2.0 copy-start
  725.8 2.0 copy-start
  733.9 3.9 copy-start.3
  733.9 3.9 copy-start.6
  733.9 3.9 copy-start.10
  733.9 4.6 copy-start.2
  733.9 4.6 copy-start.12
  733.9 4.6 copy-start.13
  733.9 4.6 copy-start.19
Sparse Core Ops, SparseCore 0:
  746.9 94.6 reduce-scatter.3
where the time goes:
time: 856 us; the launch traced here: 850 us
  waiting for transfers between devices  544 us (64%)
  local copies, waits for them, and re-layouts  140 us (16%)
  matrix products  66.6 us (8%)
  other arithmetic  44.3 us (5%)
  starting transfers between devices  38.7 us (5%)
  between operations  16.3 us (2%)
    all_to_all x1, waiting for transfers between devices, shards(): lax.all_to_all(spread_keys, 'seq', split_axis=0, concat_axis=0, tiled=True)  227 us
    ppermute x6, waiting for transfers between devices, shifted(): lax.ppermute(value, axis, [(source, source + steps) for source in range(i...  222 us
    unnamed x2, waiting for transfers between devices  94.8 us
    unnamed x56, local copies, waits for them, and re-layouts  42.6 us
    dot_general x12, matrix products, block_partial(): jnp.einsum('hqk,khd->qhd', weights.astype(jnp.bfloat16), vals, preferred_...  41.9 us
    ppermute x6, starting transfers between devices, shifted(): lax.ppermute(value, axis, [(source, source + steps) for source in range(i...  21.9 us
    dot_general x12, matrix products, block_partial(): jnp.einsum('qhd,khd->hqk', q_rows, keys, preferred_element_type=jnp.float32)  20.1 us
    lt x10, other arithmetic, visible(): return (earlier <= later) & (near | (earlier < sinks)) & valid[None, :]  17.6 us
  transfers between devices with their start and end apart: 9, of which 4 were waited for; matrix products, arithmetic and copies ran while one was open for 8% of the time, Pallas kernels for 0%

commit v1 on v0

v1 whole, which is shorter than its diff:
```python
import math

import jax
import jax.numpy as jnp
import numpy as np
from jax import lax
from jax.sharding import Mesh
from jax.sharding import PartitionSpec as P

HEAD = 128
GROUP = 4


NEG = -1e30


def visible(query_pos, key_pos, valid, window, sinks):
    later = query_pos[:, None]
    earlier = key_pos[None, :]
    near = later - earlier < window
    return (earlier <= later) & (near | (earlier < sinks)) & valid[None, :]


def block_partial(q_rows, keys, vals, query_pos, key_pos, valid, window, sinks):
    mask = visible(query_pos, key_pos, valid, window, sinks)
    scale = 1.0 / math.sqrt(q_rows.shape[-1])
    scores = jnp.einsum("qhd,khd->hqk", q_rows, keys, preferred_element_type=jnp.float32) * scale
    scores = jnp.where(mask[None], scores, NEG)
    top = jnp.max(scores, axis=2)
    weights = jnp.where(mask[None], jnp.exp(scores - top[:, :, None]), 0.0)
    total = jnp.sum(weights, axis=2)
    summed = jnp.einsum(
        "hqk,khd->qhd", weights.astype(jnp.bfloat16), vals, preferred_element_type=jnp.float32
    )
    return (summed, top.T, total.T)


def shards(
    query,
    span_keys,
    span_values,
    cache_keys,
    cache_values,
    out_weight,
    cache_lengths,
    sink_counts,
    windows,
    block_of_slot,
):
    rows, width = query.shape
    heads_here = width // HEAD
    places = lax.axis_size("place")
    group = lax.axis_size("req")
    place = lax.axis_index("place")
    mine = lax.axis_index("req")
    cache_dev = cache_keys.shape[1]
    length = cache_lengths[mine]
    window = windows[mine]
    sinks = sink_counts[mine]

    got_keys = lax.all_to_all(cache_keys, "req", split_axis=0, concat_axis=0, tiled=True)
    got_vals = lax.all_to_all(cache_values, "req", split_axis=0, concat_axis=0, tiled=True)
    span_q = lax.all_gather(query, "place", axis=0, tiled=True)

    blocks = lax.dynamic_slice_in_dim(block_of_slot[mine], place * group, group)
    slot_pos = (blocks[:, None] * cache_dev + jnp.arange(cache_dev, dtype=jnp.int32)[None, :]).reshape(-1)
    own_pos = length + place * rows + jnp.arange(rows, dtype=jnp.int32)
    query_pos = length + jnp.arange(places * rows, dtype=jnp.int32)

    keys = jnp.concatenate([got_keys.reshape(-1, width), span_keys], 0).reshape(-1, heads_here, HEAD)
    vals = jnp.concatenate([got_vals.reshape(-1, width), span_values], 0).reshape(-1, heads_here, HEAD)
    key_pos = jnp.concatenate([slot_pos, own_pos])
    valid = jnp.concatenate([slot_pos < length, jnp.ones((rows,), jnp.bool_)])

    summed, top, total = block_partial(
        span_q.reshape(-1, heads_here, HEAD), keys, vals, query_pos, key_pos, valid, window, sinks
    )
    summed = lax.all_to_all(
        summed.reshape(places, rows, width), "place", split_axis=0, concat_axis=0, tiled=True
    ).reshape(places, rows, heads_here, HEAD)
    stats = jnp.concatenate([top, total], axis=1).reshape(places, rows, 2 * heads_here)
    stats = lax.all_to_all(stats, "place", split_axis=0, concat_axis=0, tiled=True)
    top, total = stats[..., :heads_here], stats[..., heads_here:]
    best = jnp.max(top, axis=0)
    factor = jnp.exp(top - best[None])
    total = jnp.sum(total * factor, axis=0)
    summed = jnp.sum(summed * factor[..., None], axis=0)
    attention = (summed / total[..., None]).astype(jnp.bfloat16).reshape(rows, width)
    terms = jnp.dot(attention, out_weight, preferred_element_type=jnp.float32)
    return lax.psum_scatter(terms.astype(jnp.bfloat16), "tp", scatter_dimension=1, tiled=True)


def solution(mesh):
    seq_size = mesh.shape["seq"]
    requests = 8
    grid = Mesh(
        np.asarray(mesh.devices).reshape(seq_size // requests, requests, mesh.shape["tp"]),
        ("place", "req", "tp"),
    )
    seq = ("place", "req")
    return jax.shard_map(
        shards,
        mesh=grid,
        in_specs=(
            P(seq, "tp"),
            P(seq, "tp"),
            P(seq, "tp"),
            P(None, seq, "tp"),
            P(None, seq, "tp"),
            P("tp", None),
            P(),
            P(),
            P(),
            P(),
        ),
        out_specs=P(seq, "tp"),
        check_vma=False,
    )
```

time: 856 us -> 392 us (0.46)
  waiting for transfers between devices: 544 us -> 118 us
  blocking collectives: 0 us -> 139 us
  local copies, waits for them, and re-layouts: 140 us -> 38.3 us
  matrix products: 66.6 us -> 35 us
  other arithmetic: 44.3 us -> 22.6 us
  starting transfers between devices: 38.7 us -> 21.9 us
    ppermute x6 -> x0, waiting for transfers between devices: 222 us -> none  [shifted(): lax.ppermute(value, axis, [(source, source + steps) for source in range(i...]
    all_to_all x2 -> x3, waiting for transfers between devices: 227 us -> 34 us  [the longest x1 34 us: shards(): lax.all_to_all(summed.reshape(places, rows, width), 'place', split_axis=0...]
    all_gather x0 -> x1, blocking collectives: none -> 74.7 us  [shards(): span_q = lax.all_gather(query, 'place', axis=0, tiled=True)]
    all_to_all x0 -> x1, blocking collectives: none -> 64 us  [shards(): lax.all_to_all(cache_values, 'req', split_axis=0, concat_axis=0, tiled=True)]
    unnamed x56 -> x23, local copies, waits for them, and re-layouts: 42.6 us -> 6.8 us
    reshape x2 -> x4, local copies, waits for them, and re-layouts: 34.2 us -> 5.78 us  [the longest x2 5.68 us: shards(): summed.reshape(places, rows, width)]
    dot_general x12 -> x1, matrix products: 41.9 us -> 16.6 us  [block_partial(): jnp.einsum('hqk,khd->qhd', weights.astype(jnp.bfloat16), vals, preferred_...]
    all_to_all x2, local copies, waits for them, and re-layouts: 27.6 us -> 2.54 us  [the longest x1 2.03 us: shards(): lax.all_to_all(summed.reshape(places, rows, width), 'place', split_axis=0...]
  transfers between devices with their start and end apart: 9 -> 4, of which waited for: 4 -> 2; matrix products, arithmetic and copies ran while one was open for 8% -> 12% of each run, Pallas kernels for 0% -> 0%
where the time goes in v1:
time: 392 us; the launch traced here: 389 us
  blocking collectives  139 us (35%)
  waiting for transfers between devices  118 us (30%)
  local copies, waits for them, and re-layouts  38.3 us (10%)
  matrix products  35 us (9%)
  other arithmetic  22.6 us (6%)
  starting transfers between devices  21.9 us (6%)
  between operations  14.2 us (4%)
    unnamed x2, waiting for transfers between devices  84.5 us
    all_gather x1, blocking collectives, shards(): span_q = lax.all_gather(query, 'place', axis=0, tiled=True)  74.7 us
    all_to_all x1, blocking collectives, shards(): lax.all_to_all(cache_values, 'req', split_axis=0, concat_axis=0, tiled=True)  64 us
    all_to_all x1, waiting for transfers between devices, shards(): lax.all_to_all(summed.reshape(places, rows, width), 'place', split_axis=0...  34 us
    dot_general x1, matrix products, block_partial(): jnp.einsum('hqk,khd->qhd', weights.astype(jnp.bfloat16), vals, preferred_...  16.6 us
    reduce_sum x1, other arithmetic, block_partial(): total = jnp.sum(weights, axis=2)  14.2 us
    dot_general x1, matrix products, block_partial(): jnp.einsum('qhd,khd->hqk', q_rows, keys, preferred_element_type=jnp.float32)  13.8 us
    concatenate x3, local copies, waits for them, and re-layouts, shards(): jnp.concatenate([got_vals.reshape(-1, width), span_values], 0)  11.2 us
  transfers between devices with their start and end apart: 4, of which 2 were waited for; matrix products, arithmetic and copies ran while one was open for 12% of the time, Pallas kernels for 0%

profile of v1, /device:TPU:224, one launch (start us, length us, event | category | flops | bytes accessed | tf_op | source)
XLA Modules:
  0.0 389.2 jit_solution(4118115496891298422)
XLA Ops:
  6.5 64.0 %all_to_all.20 = bf16[8,256,640]{2,1,0:T(8,128)(2,1)} all-to-all(bf16[8,256,640]{2,1,0:T(8,128)(2,1)} %param.14), channel_id=1, replica_groups=mesh['place'=4,'req'=8,'tp'=8] {'req'}, dimensions={0} | all-to-all | bytes 5242880 | tf_op jit(solution)/shard_map/all_to_all | solution.py:62
  70.5 0.0 copy-start.2
  70.6 6.2 %all-to-all-start.1 = ((bf16[8,256,640]{2,1,0:T(8,128)(2,1)}), bf16[8,256,640]{2,1,0:T(8,128)(2,1)S(1)}, u32[]{:S(2)}, u32[]{:S(2)}) async-start(bf16[8,256,640]{2,1,0:T(8,128)(2,1)} %param.13), calls=%async_computation.1 | async-start | bytes 5242880 | tf_op jit(solution)/shard_map/all_to_all | solution.py:61
  76.8 0.7 dynamic_slice.15
  77.5 0.6 dynamic_slice.16
  78.1 0.7 dynamic_slice.14
  78.7 0.8 multiply_bitcast_fusion
  79.5 0.1 add_bitcast_fusion
  79.6 0.2 copy.38
  79.7 0.9 copy.40
  80.6 1.1 copy.34
  81.7 0.2 copy.36
  81.9 74.7 %all_gather.3 = bf16[768,640]{1,0:T(8,128)(2,1)} all-gather(bf16[192,640]{1,0:T(8,128)(2,1)S(1)} %copy-done.2), channel_id=1, replica_groups=mesh['place'=4,'req'=8,'tp'=8] {'place'}, dimensions={0}, use_global_device_ids=true | all-gather | bytes 1228800 | tf_op jit(solution)/shard_map/all_gather | solution.py:63
  156.6 2.3 copy.41
  159.6 0.7 broadcast_compare_fusion.1
  160.3 0.6 broadcast_compare_fusion
  160.9 0.7 iota_add_fusion
  161.6 4.6 %fusion.7 = pred[768,2240]{0,1:T(8,128)(4,1)} fusion(s32[]{:T(128)} %bitcast.3, s32[768]{0:T(1024)S(1)} %iota_add_fusion, s32[2240]{0:T(1024)S(1)} %pad_add_fusion, pred[2240]{0:T(1024)(128)(4,1)S(1)} %concatenate.33, pred[2240]{0:T(1024)(128)(4,1)S(1)} %broadcast_compare_fusion), kind=kLoop, calls=%fused_computation.9 | loop fusion | flops 10321920 | bytes 1736836 | tf_op jit(solution)/shard_map/and | solution.py:21
  166.2 7.0 %reshape.156 = bf16[2048,5,128]{2,1,0:T(8,128)(2,1)} reshape(bf16[8,256,640]{2,1,0:T(8,128)(2,1)} %all_to_all.20) | data formatting | bytes 5242880 | tf_op jit(solution)/shard_map/concatenate | solution.py:71
  173.2 4.0 %copy.35 = bf16[2048,5,128]{2,0,1:T(8,128)(2,1)} copy(bf16[2048,5,128]{2,1,0:T(8,128)(2,1)} %reshape.156) | data formatting | bytes 5242880 | tf_op jit(solution)/shard_map/concatenate | solution.py:71
  177.2 0.0 all-to-all-done.1
  177.2 4.2 %reshape.157 = bf16[2048,5,128]{2,1,0:T(8,128)(2,1)} reshape(bf16[8,256,640]{2,1,0:T(8,128)(2,1)S(1)} %all-to-all-done.1) | data formatting | bytes 5242880 | tf_op jit(solution)/shard_map/concatenate | solution.py:70
  181.4 2.7 copy.39
  184.1 0.0 copy-done
  184.1 0.3 copy-done.1
  184.4 0.0 copy-done.4
  184.4 13.8 %fusion.25 = (f32[5,768]{1,0:T(8,128)S(1)}, f32[5,768,2240]{1,2,0:T(8,128)}) fusion(bf16[768,5,128]{0,2,1:T(8,128)(2,1)S(1)} %bitcast.41, bf16[192,5,128]{2,0,1:T(8,128)(2,1)S(1)} %copy-done.4, bf16[2048,5,128]{2,0,1:T(8,128)(2,1)S(1)} %copy.39, pred[768,2240]{0,1:T(8,128)(4,1)S(1)} %copy-done), kind=kOutput, calls=%fused_computation.37 | convolution fusion | flops 2233544960 | bytes 39992320 | tf_op jit(solution)/shard_map/qhd,khd->hqk/dot_general | solution.py:27
  198.2 14.2 %fusion = f32[5,768]{1,0:T(8,128)S(1)} fusion(f32[5,768,2240]{1,2,0:T(8,128)} %get-tuple-element.8, f32[5,768]{1,0:T(8,128)S(1)} %get-tuple-element.7, pred[768,2240]{0,1:T(8,128)(4,1)S(1)} %copy-done), kind=kLoop, calls=%fused_computation.2 | loop fusion | flops 25800960 | bytes 36157440 | tf_op jit(solution)/shard_map/reduce_sum | solution.py:31
  212.4 0.1 reshape.155
  212.5 0.7 reshape.160
  213.2 7.5 %all-to-all-start.3 = ((f32[4,1,1920]{2,1,0:T(1,128)}), f32[4,1,1920]{2,1,0:T(1,128)S(1)}, u32[]{:S(2)}, u32[]{:S(2)}) async-start(f32[4,1,1920]{2,1,0:T(1,128)} %reshape.160), calls=%async_computation.3 | async-start | bytes 61440 | tf_op jit(solution)/shard_map/all_to_all | solution.py:82
  220.8 16.6 %fusion.15 = f32[768,5,128]{0,2,1:T(8,128)} fusion(f32[5,768,2240]{1,2,0:T(8,128)} %get-tuple-element.8, f32[5,768]{1,0:T(8,128)S(1)} %get-tuple-element.7, pred[768,2240]{0,1:T(8,128)(4,1)S(1)} %copy-done, bf16[192,5,128]{2,0,1:T(8,128)(2,1)S(1)} %copy.36, bf16[2048,5,128]{2,0,1:T(8,128)(2,1)} %copy.35), kind=kOutput, calls=%fused_computation.19 | convolution fusion | flops 2233548800 | bytes 40975360 | tf_op jit(solution)/shard_map/hqk,khd->qhd/dot_general | solution.py:32
  237.4 3.1 reshape.154
  240.5 2.5 copy.43
  243.1 0.0 all-to-all-done.3
  243.1 8.1 %all-to-all-start.2 = ((f32[4,192,640]{2,1,0:T(8,128)}), f32[4,192,640]{2,1,0:T(8,128)}, u32[]{:S(2)}, u32[]{:S(2)}) async-start(f32[4,192,640]{2,1,0:T(8,128)} %copy.43), calls=%async_computation.2 | async-start | bytes 3932160 | tf_op jit(solution)/shard_map/all_to_all | solution.py:78
  251.2 0.5 broadcast.100
  251.7 0.7 reduce.1
  252.4 0.1 reshape.161
  252.6 34.0 %all-to-all-done.2 = f32[4,192,640]{2,1,0:T(8,128)} async-done(((f32[4,192,640]{2,1,0:T(8,128)}), f32[4,192,640]{2,1,0:T(8,128)}, u32[]{:S(2)}, u32[]{:S(2)}) %all-to-all-start.2) | async-done | bytes 1966112 | tf_op jit(solution)/shard_map/all_to_all | solution.py:78
  286.6 2.0 copy.45
  288.6 0.2 fusion.14
  288.9 0.1 fusion.20
  288.9 4.6 %convolution_convert_fusion = bf16[192,5120]{1,0:T(8,128)(2,1)S(1)} fusion(bf16[192,640]{0,1:T(8,128)(2,1)S(1)} %fusion.20, bf16[640,5120]{1,0:T(8,128)(2,1)} %param.15), kind=kOutput, calls=%fused_computation.10 | convolution fusion | flops 1259274240 | bytes 8765440 | tf_op jit(solution)/shard_map/dot_general | solution.py:89
  293.5 2.6 copy.51
  296.1 0.0 reduce-scatter.4.cloned.1.call-update
  296.1 84.4 %reduce-scatter.4.cloned.1.call-done = bf16[640,192]{1,0:T(8,128)(2,1)} async-done(((bf16[5120,192]{1,0:T(8,128)(2,1)}), bf16[640,192]{1,0:T(8,128)(2,1)}) %reduce-scatter.4.cloned.1.call-update) | async-done | bytes 245776
  380.6 1.8 copy.52
  (21 shorter events, 0.1 us)
Async XLA Ops:
  70.5 6.3 %copy-start.5 = (s32[8]{0:T(128)S(1)}, s32[8]{0:T(128)}, u32[]{:S(2)}) copy-start(s32[8]{0:T(128)} %param.18) | copy-start | bytes 100
  70.5 6.9 %copy-start.6 = (s32[8]{0:T(128)S(1)}, s32[8]{0:T(128)}, u32[]{:S(2)}) copy-start(s32[8]{0:T(128)} %param.17) | copy-start | bytes 100
  70.5 7.5 %copy-start.7 = (s32[8]{0:T(128)S(1)}, s32[8]{0:T(128)}, u32[]{:S(2)}) copy-start(s32[8]{0:T(128)} %param.16) | copy-start | bytes 100
  70.5 9.0 %copy-start.3 = (bf16[192,640]{1,0:T(8,128)(2,1)S(1)}, bf16[192,640]{1,0:T(8,128)(2,1)}, u32[]{:S(2)}) copy-start(bf16[192,640]{1,0:T(8,128)(2,1)} %param.11) | copy-start | bytes 737284
  70.5 11.4 %copy-start.2 = (bf16[192,640]{1,0:T(8,128)(2,1)S(1)}, bf16[192,640]{1,0:T(8,128)(2,1)}, u32[]{:S(2)}) copy-start(bf16[192,640]{1,0:T(8,128)(2,1)} %param.10) | copy-start | bytes 737284
  70.6 106.7 %all-to-all-start.1 = ((bf16[8,256,640]{2,1,0:T(8,128)(2,1)}), bf16[8,256,640]{2,1,0:T(8,128)(2,1)S(1)}, u32[]{:S(2)}, u32[]{:S(2)}) async-start(bf16[8,256,640]{2,1,0:T(8,128)(2,1)} %param.13), calls=%async_computation.1 | async-start | bytes 5242880 | tf_op jit(solution)/shard_map/all_to_all | solution.py:61
  181.4 2.7 copy-start
  181.4 3.0 copy-start.1
  181.4 3.0 copy-start.4
  213.2 29.8 %all-to-all-start.3 = ((f32[4,1,1920]{2,1,0:T(1,128)}), f32[4,1,1920]{2,1,0:T(1,128)S(1)}, u32[]{:S(2)}, u32[]{:S(2)}) async-start(f32[4,1,1920]{2,1,0:T(1,128)} %reshape.160), calls=%async_computation.3 | async-start | bytes 61440 | tf_op jit(solution)/shard_map/all_to_all | solution.py:82
  243.1 43.5 %all-to-all-start.2 = ((f32[4,192,640]{2,1,0:T(8,128)}), f32[4,192,640]{2,1,0:T(8,128)}, u32[]{:S(2)}, u32[]{:S(2)}) async-start(f32[4,192,640]{2,1,0:T(8,128)} %copy.43), calls=%async_computation.2 | async-start | bytes 3932160 | tf_op jit(solution)/shard_map/all_to_all | solution.py:78
  251.2 129.4 %reduce-scatter.4.cloned.1.call-start = ((), (), s32[]{:S(2)}) async-start(), calls=%async_computation.5 | async-start | bytes 2949120
Sparse Core Ops, SparseCore 0:
  296.2 84.2 reduce-scatter.3

commit v2 on v1

--- a/solution.py
+++ b/solution.py
@@ -60,7 +60,9 @@
 
     got_keys = lax.all_to_all(cache_keys, "req", split_axis=0, concat_axis=0, tiled=True)
     got_vals = lax.all_to_all(cache_values, "req", split_axis=0, concat_axis=0, tiled=True)
-    span_q = lax.all_gather(query, "place", axis=0, tiled=True)
+    span_q = lax.all_to_all(
+        jnp.broadcast_to(query[None], (places,) + query.shape), "place", split_axis=0, concat_axis=0, tiled=True
+    )
 
     blocks = lax.dynamic_slice_in_dim(block_of_slot[mine], place * group, group)
     slot_pos = (blocks[:, None] * cache_dev + jnp.arange(cache_dev, dtype=jnp.int32)[None, :]).reshape(-1)
@@ -86,8 +88,12 @@
     total = jnp.sum(total * factor, axis=0)
     summed = jnp.sum(summed * factor[..., None], axis=0)
     attention = (summed / total[..., None]).astype(jnp.bfloat16).reshape(rows, width)
-    terms = jnp.dot(attention, out_weight, preferred_element_type=jnp.float32)
-    return lax.psum_scatter(terms.astype(jnp.bfloat16), "tp", scatter_dimension=1, tiled=True)
+    parts = lax.axis_size("tp")
+    terms = jnp.einsum(
+        "qf,fkc->kqc", attention, out_weight.reshape(width, parts, -1), preferred_element_type=jnp.float32
+    )
+    terms = lax.all_to_all(terms.astype(jnp.bfloat16), "tp", split_axis=0, concat_axis=0, tiled=True)
+    return jnp.sum(terms.astype(jnp.float32), axis=0).astype(jnp.bfloat16)
 
 
 def solution(mesh):

time: 392 us -> 296 us (0.76)
  blocking collectives: 139 us -> 54.9 us
  starting transfers between devices: 21.9 us -> 36.5 us
  between operations: 14.2 us -> 0.73 us
  waiting for transfers between devices: 118 us -> 107 us
    unnamed x2 -> x0, waiting for transfers between devices: 84.5 us -> none
    all_gather x1 -> x0, blocking collectives: 74.7 us -> none  [shards(): span_q = lax.all_gather(query, 'place', axis=0, tiled=True)]
    all_to_all x1, waiting for transfers between devices: 0.01 us -> 51.4 us  [shards(): lax.all_to_all(cache_keys, 'req', split_axis=0, concat_axis=0, tiled=True)]
    all_to_all x0 -> x1, waiting for transfers between devices: none -> 12.9 us  [shards(): lax.all_to_all(cache_values, 'req', split_axis=0, concat_axis=0, tiled=True)]
    all_to_all x1 -> x2, blocking collectives: 64 us -> 54.9 us  [the longest x1 32.2 us: shards(): lax.all_to_all(terms.astype(jnp.bfloat16), 'tp', split_axis=0, concat_axi...]
    all_to_all x1, waiting for transfers between devices: 34 us -> 42.9 us  [shards(): lax.all_to_all(summed.reshape(places, rows, width), 'place', split_axis=0...]
    all_to_all x1, starting transfers between devices: 6.25 us -> 13.2 us  [shards(): lax.all_to_all(cache_keys, 'req', split_axis=0, concat_axis=0, tiled=True)]
    all_to_all x0 -> x1, starting transfers between devices: none -> 6.86 us  [shards(): lax.all_to_all(cache_values, 'req', split_axis=0, concat_axis=0, tiled=True)]
  transfers between devices with their start and end apart: 4 -> 4, of which waited for: 2 -> 3; matrix products, arithmetic and copies ran while one was open for 12% -> 29% of each run, Pallas kernels for 0% -> 0%
where the time goes in v2:
time: 296 us; the launch traced here: 293 us
  waiting for transfers between devices  107 us (36%)
  blocking collectives  54.9 us (19%)
  starting transfers between devices  36.5 us (12%)
  matrix products  35.5 us (12%)
  local copies, waits for them, and re-layouts  35.3 us (12%)
  other arithmetic  23.4 us (8%)
    all_to_all x1, waiting for transfers between devices, shards(): lax.all_to_all(cache_keys, 'req', split_axis=0, concat_axis=0, tiled=True)  51.4 us
    all_to_all x1, waiting for transfers between devices, shards(): lax.all_to_all(summed.reshape(places, rows, width), 'place', split_axis=0...  42.9 us
    all_to_all x1, blocking collectives, shards(): lax.all_to_all(terms.astype(jnp.bfloat16), 'tp', split_axis=0, concat_axi...  32.2 us
    all_to_all x1, blocking collectives, shards(): lax.all_to_all(jnp.broadcast_to(query[None], (places,) + query.shape), 'p...  22.7 us
    dot_general x1, matrix products, block_partial(): jnp.einsum('hqk,khd->qhd', weights.astype(jnp.bfloat16), vals, preferred_...  16.6 us
    dot_general x1, matrix products, block_partial(): jnp.einsum('qhd,khd->hqk', q_rows, keys, preferred_element_type=jnp.float32)  14.3 us
    reduce_sum x1, other arithmetic, block_partial(): total = jnp.sum(weights, axis=2)  14.2 us
    all_to_all x1, starting transfers between devices, shards(): lax.all_to_all(cache_keys, 'req', split_axis=0, concat_axis=0, tiled=True)  13.2 us
  transfers between devices with their start and end apart: 4, of which 3 were waited for; matrix products, arithmetic and copies ran while one was open for 29% of the time, Pallas kernels for 0%

profile of v2, /device:TPU:224, one launch (start us, length us, event | category | flops | bytes accessed | tf_op | source)
XLA Modules:
  0.0 293.5 jit_solution(13107189024407590836)
XLA Ops:
  0.0 1.0 broadcast_in_dim.21
  1.0 22.7 %all_to_all.30 = bf16[4,192,640]{2,1,0:T(8,128)(2,1)} all-to-all(bf16[4,192,640]{2,1,0:T(8,128)(2,1)S(1)} %broadcast_in_dim.21), channel_id=1, replica_groups=mesh['place'=4,'req'=8,'tp'=8] {'place'}, dimensions={0} | all-to-all | bytes 1966080 | tf_op jit(solution)/shard_map/all_to_all | solution.py:63
  23.7 0.0 copy-start.3
  23.7 13.2 %all-to-all-start.1 = ((bf16[8,256,640]{2,1,0:T(8,128)(2,1)}), bf16[8,256,640]{2,1,0:T(8,128)(2,1)S(1)}, u32[]{:S(2)}, u32[]{:S(2)}) async-start(bf16[8,256,640]{2,1,0:T(8,128)(2,1)} %param.13), calls=%async_computation.1 | async-start | bytes 5242880 | tf_op jit(solution)/shard_map/all_to_all | solution.py:61
  36.9 0.8 multiply_bitcast_fusion
  37.7 0.1 add_bitcast_fusion
  37.7 0.6 dynamic_slice.14
  38.3 0.6 dynamic_slice.16
  38.9 0.6 dynamic_slice.15
  39.5 0.2 copy.43
  39.7 0.9 copy.45
  40.6 0.2 copy.39
  40.8 0.2 copy.41
  41.5 0.6 broadcast_compare_fusion.1
  42.1 0.6 broadcast_compare_fusion
  42.7 0.6 iota_add_fusion
  43.3 51.4 %all-to-all-done.1 = bf16[8,256,640]{2,1,0:T(8,128)(2,1)S(1)} async-done(((bf16[8,256,640]{2,1,0:T(8,128)(2,1)}), bf16[8,256,640]{2,1,0:T(8,128)(2,1)S(1)}, u32[]{:S(2)}, u32[]{:S(2)}) %all-to-all-start.1) | async-done | bytes 2621472 | tf_op jit(solution)/shard_map/all_to_all | solution.py:61
  94.6 6.9 %all-to-all-start = ((bf16[8,256,640]{2,1,0:T(8,128)(2,1)}), bf16[8,256,640]{2,1,0:T(8,128)(2,1)}, u32[]{:S(2)}, u32[]{:S(2)}) async-start(bf16[8,256,640]{2,1,0:T(8,128)(2,1)} %param.14), calls=%async_computation | async-start | bytes 5242880 | tf_op jit(solution)/shard_map/all_to_all | solution.py:62
  101.5 4.6 %fusion.7 = pred[768,2240]{0,1:T(8,128)(4,1)} fusion(s32[]{:T(128)} %bitcast.3, s32[768]{0:T(1024)S(1)} %iota_add_fusion, s32[2240]{0:T(1024)S(1)} %pad_add_fusion, pred[2240]{0:T(1024)(128)(4,1)S(1)} %concatenate.33, pred[2240]{0:T(1024)(128)(4,1)S(1)} %broadcast_compare_fusion), kind=kLoop, calls=%fused_computation.9 | loop fusion | flops 10321920 | bytes 1736836 | tf_op jit(solution)/shard_map/and | solution.py:21
  106.1 3.5 %reshape.173 = bf16[768,5,128]{2,1,0:T(8,128)(2,1)} reshape(bf16[4,192,640]{2,1,0:T(8,128)(2,1)} %all_to_all.30) | data formatting | bytes 1966080 | tf_op jit(solution)/shard_map/reshape | solution.py:78
  109.6 4.2 %reshape.172 = bf16[2048,5,128]{2,1,0:T(8,128)(2,1)} reshape(bf16[8,256,640]{2,1,0:T(8,128)(2,1)S(1)} %all-to-all-done.1) | data formatting | bytes 5242880 | tf_op jit(solution)/shard_map/concatenate | solution.py:72
  113.8 2.7 copy.44
  116.5 0.0 copy-done
  116.5 0.5 copy-done.1
  117.0 0.0 copy-done.4
  117.0 14.3 %fusion.30 = (f32[5,768]{1,0:T(8,128)S(1)}, f32[5,768,2240]{1,2,0:T(8,128)}) fusion(bf16[768,5,128]{2,1,0:T(8,128)(2,1)S(1)} %copy-done.1, bf16[192,5,128]{2,0,1:T(8,128)(2,1)S(1)} %copy-done.4, bf16[2048,5,128]{2,0,1:T(8,128)(2,1)S(1)} %copy.44, pred[768,2240]{0,1:T(8,128)(4,1)S(1)} %copy-done), kind=kOutput, calls=%fused_computation.40 | convolution fusion | flops 2233544960 | bytes 39992320 | tf_op jit(solution)/shard_map/qhd,khd->hqk/dot_general | solution.py:27
  131.4 14.2 %fusion = f32[5,768]{1,0:T(8,128)S(1)} fusion(f32[5,768,2240]{1,2,0:T(8,128)} %get-tuple-element.8, f32[5,768]{1,0:T(8,128)S(1)} %get-tuple-element.7, pred[768,2240]{0,1:T(8,128)(4,1)S(1)} %copy-done), kind=kLoop, calls=%fused_computation.2 | loop fusion | flops 25800960 | bytes 36157440 | tf_op jit(solution)/shard_map/reduce_sum | solution.py:31
  145.6 0.1 reshape.168
  145.7 0.7 reshape.174
  146.4 12.9 %all-to-all-done = bf16[8,256,640]{2,1,0:T(8,128)(2,1)} async-done(((bf16[8,256,640]{2,1,0:T(8,128)(2,1)}), bf16[8,256,640]{2,1,0:T(8,128)(2,1)}, u32[]{:S(2)}, u32[]{:S(2)}) %all-to-all-start) | async-done | bytes 2621472 | tf_op jit(solution)/shard_map/all_to_all | solution.py:62
  159.3 8.3 %all-to-all-start.4 = ((f32[4,1,1920]{2,1,0:T(1,128)}), f32[4,1,1920]{2,1,0:T(1,128)S(1)}, u32[]{:S(2)}, u32[]{:S(2)}) async-start(f32[4,1,1920]{2,1,0:T(1,128)} %reshape.174), calls=%async_computation.4 | async-start | bytes 61440 | tf_op jit(solution)/shard_map/all_to_all | solution.py:84
  167.7 7.0 %reshape.171 = bf16[2048,5,128]{2,1,0:T(8,128)(2,1)} reshape(bf16[8,256,640]{2,1,0:T(8,128)(2,1)} %all-to-all-done) | data formatting | bytes 5242880 | tf_op jit(solution)/shard_map/concatenate | solution.py:73
  174.6 4.0 %copy.40 = bf16[2048,5,128]{2,0,1:T(8,128)(2,1)} copy(bf16[2048,5,128]{2,1,0:T(8,128)(2,1)} %reshape.171) | data formatting | bytes 5242880 | tf_op jit(solution)/shard_map/concatenate | solution.py:73
  178.7 16.6 %fusion.20 = f32[768,5,128]{0,2,1:T(8,128)} fusion(f32[5,768,2240]{1,2,0:T(8,128)} %get-tuple-element.8, f32[5,768]{1,0:T(8,128)S(1)} %copy-done.6, pred[768,2240]{0,1:T(8,128)(4,1)S(1)} %copy-done, bf16[192,5,128]{2,0,1:T(8,128)(2,1)S(1)} %copy.41, bf16[2048,5,128]{2,0,1:T(8,128)(2,1)} %copy.40), kind=kOutput, calls=%fused_computation.22 | convolution fusion | flops 2233548800 | bytes 40975360 | tf_op jit(solution)/shard_map/hqk,khd->qhd/dot_general | solution.py:32
  195.2 3.1 %reshape.167 = f32[4,192,640]{1,0,2:T(4,128)S(1)} reshape(f32[768,5,128]{0,2,1:T(8,128)} %fusion.20) | data formatting | bytes 3932160 | tf_op jit(solution)/shard_map/reshape | solution.py:81
  198.4 2.5 copy.48
  200.9 0.0 all-to-all-done.4
  200.9 8.1 %all-to-all-start.3 = ((f32[4,192,640]{2,1,0:T(8,128)}), f32[4,192,640]{2,1,0:T(8,128)}, u32[]{:S(2)}, u32[]{:S(2)}) async-start(f32[4,192,640]{2,1,0:T(8,128)} %copy.48), calls=%async_computation.3 | async-start | bytes 3932160 | tf_op jit(solution)/shard_map/all_to_all | solution.py:80
  209.0 0.5 broadcast.104
  209.5 0.7 reduce.2
  210.2 0.1 reshape.175
  210.4 42.9 %all-to-all-done.3 = f32[4,192,640]{2,1,0:T(8,128)} async-done(((f32[4,192,640]{2,1,0:T(8,128)}), f32[4,192,640]{2,1,0:T(8,128)}, u32[]{:S(2)}, u32[]{:S(2)}) %all-to-all-start.3) | async-done | bytes 1966112 | tf_op jit(solution)/shard_map/all_to_all | solution.py:80
  253.3 2.0 copy.50
  255.4 0.2 fusion.17
  255.6 0.1 divide_convert_fusion
  255.7 4.6 %convert_bitcast_fusion = bf16[8,192,640]{2,1,0:T(8,128)(2,1)S(1)} fusion(bf16[192,640,1]{0,1,2:T(8,128)(2,1)S(1)} %bitcast.46, bf16[80,8,8,640]{3,2,1,0:T(8,128)(2,1)} %bitcast.53), kind=kOutput, calls=%fused_computation.21 | convolution fusion | flops 1259274240 | bytes 8765440 | tf_op jit(solution)/shard_map/qf,fkc->kqc/dot_general | solution.py:92
  260.3 32.2 %all_to_all.31 = bf16[8,192,640]{2,1,0:T(8,128)(2,1)S(1)} all-to-all(bf16[8,192,640]{2,1,0:T(8,128)(2,1)S(1)} %convert_bitcast_fusion), channel_id=1, replica_groups=mesh['place'=4,'req'=8,'tp'=8] {'tp'}, dimensions={0} | all-to-all | bytes 3932160 | tf_op jit(solution)/shard_map/all_to_all | solution.py:95
  292.5 1.0 reduce_sum.45
  (24 shorter events, 0.1 us)
Async XLA Ops:
  23.7 14.0 %copy-start.7 = (s32[8]{0:T(128)S(1)}, s32[8]{0:T(128)}, u32[]{:S(2)}) copy-start(s32[8]{0:T(128)} %param.16) | copy-start | bytes 100
  23.7 14.6 %copy-start.8 = (s32[8]{0:T(128)S(1)}, s32[8]{0:T(128)}, u32[]{:S(2)}) copy-start(s32[8]{0:T(128)} %param.17) | copy-start | bytes 100
  23.7 15.2 %copy-start.9 = (s32[8]{0:T(128)S(1)}, s32[8]{0:T(128)}, u32[]{:S(2)}) copy-start(s32[8]{0:T(128)} %param.18) | copy-start | bytes 100
  23.7 15.8 %copy-start.2 = (bf16[192,640]{1,0:T(8,128)(2,1)S(1)}, bf16[192,640]{1,0:T(8,128)(2,1)}, u32[]{:S(2)}) copy-start(bf16[192,640]{1,0:T(8,128)(2,1)} %param.11) | copy-start | bytes 737284
  23.7 16.9 %copy-start.3 = (bf16[192,640]{1,0:T(8,128)(2,1)S(1)}, bf16[192,640]{1,0:T(8,128)(2,1)}, u32[]{:S(2)}) copy-start(bf16[192,640]{1,0:T(8,128)(2,1)} %param.12) | copy-start | bytes 737284
  23.7 70.9 %all-to-all-start.1 = ((bf16[8,256,640]{2,1,0:T(8,128)(2,1)}), bf16[8,256,640]{2,1,0:T(8,128)(2,1)S(1)}, u32[]{:S(2)}, u32[]{:S(2)}) async-start(bf16[8,256,640]{2,1,0:T(8,128)(2,1)} %param.13), calls=%async_computation.1 | async-start | bytes 5242880 | tf_op jit(solution)/shard_map/all_to_all | solution.py:61
  94.6 64.7 %all-to-all-start = ((bf16[8,256,640]{2,1,0:T(8,128)(2,1)}), bf16[8,256,640]{2,1,0:T(8,128)(2,1)}, u32[]{:S(2)}, u32[]{:S(2)}) async-start(bf16[8,256,640]{2,1,0:T(8,128)(2,1)} %param.14), calls=%async_computation | async-start | bytes 5242880 | tf_op jit(solution)/shard_map/all_to_all | solution.py:62
  113.8 2.7 copy-start
  113.8 3.2 %copy-start.1 = (bf16[768,5,128]{2,1,0:T(8,128)(2,1)S(1)}, bf16[768,5,128]{2,1,0:T(8,128)(2,1)}, u32[]{:S(2)}) copy-start(bf16[768,5,128]{2,1,0:T(8,128)(2,1)} %reshape.173) | copy-start | bytes 2949124
  113.8 3.2 %copy-start.4 = (bf16[192,5,128]{2,0,1:T(8,128)(2,1)S(1)}, bf16[192,5,128]{2,0,1:T(8,128)(2,1)}, u32[]{:S(2)}) copy-start(bf16[192,5,128]{2,0,1:T(8,128)(2,1)} %copy.45) | copy-start | bytes 737284
  131.3 14.2 %copy-start.5 = (f32[5,768]{1,0:T(8,128)}, f32[5,768]{1,0:T(8,128)S(1)}, u32[]{:S(2)}) copy-start(f32[5,768]{1,0:T(8,128)S(1)} %get-tuple-element.7) | copy-start | bytes 46084
  159.3 41.6 %all-to-all-start.4 = ((f32[4,1,1920]{2,1,0:T(1,128)}), f32[4,1,1920]{2,1,0:T(1,128)S(1)}, u32[]{:S(2)}, u32[]{:S(2)}) async-start(f32[4,1,1920]{2,1,0:T(1,128)} %reshape.174), calls=%async_computation.4 | async-start | bytes 61440 | tf_op jit(solution)/shard_map/all_to_all | solution.py:84
  174.6 4.0 %copy-start.6 = (f32[5,768]{1,0:T(8,128)S(1)}, f32[5,768]{1,0:T(8,128)}, u32[]{:S(2)}) copy-start(f32[5,768]{1,0:T(8,128)} %copy-done.5) | copy-start | bytes 46084
  200.9 52.4 %all-to-all-start.3 = ((f32[4,192,640]{2,1,0:T(8,128)}), f32[4,192,640]{2,1,0:T(8,128)}, u32[]{:S(2)}, u32[]{:S(2)}) async-start(f32[4,192,640]{2,1,0:T(8,128)} %copy.48), calls=%async_computation.3 | async-start | bytes 3932160 | tf_op jit(solution)/shard_map/all_to_all | solution.py:80

commit v3 on v2

--- a/solution.py
+++ b/solution.py
@@ -78,8 +78,8 @@
         span_q.reshape(-1, heads_here, HEAD), keys, vals, query_pos, key_pos, valid, window, sinks
     )
     summed = lax.all_to_all(
-        summed.reshape(places, rows, width), "place", split_axis=0, concat_axis=0, tiled=True
-    ).reshape(places, rows, heads_here, HEAD)
+        summed.astype(jnp.bfloat16).reshape(places, rows, width), "place", split_axis=0, concat_axis=0, tiled=True
+    ).reshape(places, rows, heads_here, HEAD).astype(jnp.float32)
     stats = jnp.concatenate([top, total], axis=1).reshape(places, rows, 2 * heads_here)
     stats = lax.all_to_all(stats, "place", split_axis=0, concat_axis=0, tiled=True)
     top, total = stats[..., :heads_here], stats[..., heads_here:]

time: 296 us -> 270 us (0.912)
  waiting for transfers between devices: 107 us -> 85.9 us
  local copies, waits for them, and re-layouts: 35.3 us -> 31.7 us
    all_to_all x1, waiting for transfers between devices: 42.9 us -> 21.6 us  [shards(): lax.all_to_all(summed.astype(jnp.bfloat16).reshape(places, rows, width),...]
  transfers between devices with their start and end apart: 4 -> 4, of which waited for: 3 -> 3; matrix products, arithmetic and copies ran while one was open for 29% -> 30% of each run, Pallas kernels for 0% -> 0%
where the time goes in v3:
time: 270 us; the launch traced here: 267 us
  waiting for transfers between devices  85.9 us (32%)
  blocking collectives  54.9 us (20%)
  starting transfers between devices  36.5 us (14%)
  matrix products  34.2 us (13%)
  local copies, waits for them, and re-layouts  31.7 us (12%)
  other arithmetic  23.5 us (9%)
    all_to_all x1, waiting for transfers between devices, shards(): lax.all_to_all(cache_keys, 'req', split_axis=0, concat_axis=0, tiled=True)  51.4 us
    all_to_all x1, blocking collectives, shards(): lax.all_to_all(terms.astype(jnp.bfloat16), 'tp', split_axis=0, concat_axi...  32.2 us
    all_to_all x1, blocking collectives, shards(): lax.all_to_all(jnp.broadcast_to(query[None], (places,) + query.shape), 'p...  22.7 us
    all_to_all x1, waiting for transfers between devices, shards(): lax.all_to_all(summed.astype(jnp.bfloat16).reshape(places, rows, width),...  21.6 us
    dot_general x1, matrix products, block_partial(): jnp.einsum('hqk,khd->qhd', weights.astype(jnp.bfloat16), vals, preferred_...  15.2 us
    dot_general x1, matrix products, block_partial(): jnp.einsum('qhd,khd->hqk', q_rows, keys, preferred_element_type=jnp.float32)  14.3 us
    reduce_sum x1, other arithmetic, block_partial(): total = jnp.sum(weights, axis=2)  14.2 us
    all_to_all x1, starting transfers between devices, shards(): lax.all_to_all(cache_keys, 'req', split_axis=0, concat_axis=0, tiled=True)  13.2 us
  transfers between devices with their start and end apart: 4, of which 3 were waited for; matrix products, arithmetic and copies ran while one was open for 30% of the time, Pallas kernels for 0%

profile of v3, /device:TPU:224, one launch (start us, length us, event | category | flops | bytes accessed | tf_op | source)
XLA Modules:
  0.0 267.3 jit_solution(17543245346537702226)
XLA Ops:
  0.0 1.0 broadcast_in_dim.21
  1.0 22.7 %all_to_all.30 = bf16[4,192,640]{2,1,0:T(8,128)(2,1)} all-to-all(bf16[4,192,640]{2,1,0:T(8,128)(2,1)S(1)} %broadcast_in_dim.21), channel_id=1, replica_groups=mesh['place'=4,'req'=8,'tp'=8] {'place'}, dimensions={0} | all-to-all | bytes 1966080 | tf_op jit(solution)/shard_map/all_to_all | solution.py:63
  23.7 0.0 copy-start.3
  23.7 13.2 %all-to-all-start.1 = ((bf16[8,256,640]{2,1,0:T(8,128)(2,1)}), bf16[8,256,640]{2,1,0:T(8,128)(2,1)S(1)}, u32[]{:S(2)}, u32[]{:S(2)}) async-start(bf16[8,256,640]{2,1,0:T(8,128)(2,1)} %param.13), calls=%async_computation.1 | async-start | bytes 5242880 | tf_op jit(solution)/shard_map/all_to_all | solution.py:61
  36.9 0.8 multiply_bitcast_fusion
  37.7 0.1 add_bitcast_fusion
  37.7 0.6 dynamic_slice.14
  38.3 0.6 dynamic_slice.16
  38.9 0.6 dynamic_slice.15
  39.5 0.2 copy.43
  39.7 0.9 copy.45
  40.6 0.2 copy.39
  40.8 0.2 copy.41
  41.5 0.6 broadcast_compare_fusion.1
  42.1 0.6 broadcast_compare_fusion
  42.7 0.6 iota_add_fusion
  43.3 51.4 %all-to-all-done.1 = bf16[8,256,640]{2,1,0:T(8,128)(2,1)S(1)} async-done(((bf16[8,256,640]{2,1,0:T(8,128)(2,1)}), bf16[8,256,640]{2,1,0:T(8,128)(2,1)S(1)}, u32[]{:S(2)}, u32[]{:S(2)}) %all-to-all-start.1) | async-done | bytes 2621472 | tf_op jit(solution)/shard_map/all_to_all | solution.py:61
  94.6 6.9 %all-to-all-start = ((bf16[8,256,640]{2,1,0:T(8,128)(2,1)}), bf16[8,256,640]{2,1,0:T(8,128)(2,1)}, u32[]{:S(2)}, u32[]{:S(2)}) async-start(bf16[8,256,640]{2,1,0:T(8,128)(2,1)} %param.14), calls=%async_computation | async-start | bytes 5242880 | tf_op jit(solution)/shard_map/all_to_all | solution.py:62
  101.5 4.6 %fusion.7 = pred[768,2240]{0,1:T(8,128)(4,1)} fusion(s32[]{:T(128)} %bitcast.3, s32[768]{0:T(1024)S(1)} %iota_add_fusion, s32[2240]{0:T(1024)S(1)} %pad_add_fusion, pred[2240]{0:T(1024)(128)(4,1)S(1)} %concatenate.33, pred[2240]{0:T(1024)(128)(4,1)S(1)} %broadcast_compare_fusion), kind=kLoop, calls=%fused_computation.9 | loop fusion | flops 10321920 | bytes 1736836 | tf_op jit(solution)/shard_map/and | solution.py:21
  106.1 3.5 %reshape.173 = bf16[768,5,128]{2,1,0:T(8,128)(2,1)} reshape(bf16[4,192,640]{2,1,0:T(8,128)(2,1)} %all_to_all.30) | data formatting | bytes 1966080 | tf_op jit(solution)/shard_map/reshape | solution.py:78
  109.6 4.2 %reshape.172 = bf16[2048,5,128]{2,1,0:T(8,128)(2,1)} reshape(bf16[8,256,640]{2,1,0:T(8,128)(2,1)S(1)} %all-to-all-done.1) | data formatting | bytes 5242880 | tf_op jit(solution)/shard_map/concatenate | solution.py:72
  113.8 2.7 %copy.44 = bf16[2048,5,128]{2,0,1:T(8,128)(2,1)S(1)} copy(bf16[2048,5,128]{2,1,0:T(8,128)(2,1)} %reshape.172) | data formatting | bytes 5242880 | tf_op jit(solution)/shard_map/concatenate | solution.py:72
  116.5 0.0 copy-done
  116.5 0.5 copy-done.1
  117.0 0.0 copy-done.4
  117.0 14.3 %fusion.35 = (f32[5,768]{1,0:T(8,128)S(1)}, f32[5,768,2240]{1,2,0:T(8,128)}) fusion(bf16[768,5,128]{2,1,0:T(8,128)(2,1)S(1)} %copy-done.1, bf16[192,5,128]{2,0,1:T(8,128)(2,1)S(1)} %copy-done.4, bf16[2048,5,128]{2,0,1:T(8,128)(2,1)S(1)} %copy.44, pred[768,2240]{0,1:T(8,128)(4,1)S(1)} %copy-done), kind=kOutput, calls=%fused_computation.41 | convolution fusion | flops 2233544960 | bytes 39992320 | tf_op jit(solution)/shard_map/qhd,khd->hqk/dot_general | solution.py:27
  131.4 14.2 %fusion = f32[5,768]{1,0:T(8,128)S(1)} fusion(f32[5,768,2240]{1,2,0:T(8,128)} %get-tuple-element.8, f32[5,768]{1,0:T(8,128)S(1)} %get-tuple-element.7, pred[768,2240]{0,1:T(8,128)(4,1)S(1)} %copy-done), kind=kLoop, calls=%fused_computation.2 | loop fusion | flops 25800960 | bytes 36157440 | tf_op jit(solution)/shard_map/reduce_sum | solution.py:31
  145.6 0.1 reshape.168
  145.7 0.7 reshape.174
  146.4 12.9 %all-to-all-done = bf16[8,256,640]{2,1,0:T(8,128)(2,1)} async-done(((bf16[8,256,640]{2,1,0:T(8,128)(2,1)}), bf16[8,256,640]{2,1,0:T(8,128)(2,1)}, u32[]{:S(2)}, u32[]{:S(2)}) %all-to-all-start) | async-done | bytes 2621472 | tf_op jit(solution)/shard_map/all_to_all | solution.py:62
  159.3 8.3 %all-to-all-start.4 = ((f32[4,1,1920]{2,1,0:T(1,128)}), f32[4,1,1920]{2,1,0:T(1,128)S(1)}, u32[]{:S(2)}, u32[]{:S(2)}) async-start(f32[4,1,1920]{2,1,0:T(1,128)} %reshape.174), calls=%async_computation.4 | async-start | bytes 61440 | tf_op jit(solution)/shard_map/all_to_all | solution.py:84
  167.7 7.0 %reshape.171 = bf16[2048,5,128]{2,1,0:T(8,128)(2,1)} reshape(bf16[8,256,640]{2,1,0:T(8,128)(2,1)} %all-to-all-done) | data formatting | bytes 5242880 | tf_op jit(solution)/shard_map/concatenate | solution.py:73
  174.6 4.0 %copy.40 = bf16[2048,5,128]{2,0,1:T(8,128)(2,1)} copy(bf16[2048,5,128]{2,1,0:T(8,128)(2,1)} %reshape.171) | data formatting | bytes 5242880 | tf_op jit(solution)/shard_map/concatenate | solution.py:73
  178.7 15.2 %fusion.25 = bf16[768,5,128]{0,2,1:T(8,128)(2,1)S(1)} fusion(f32[5,768,2240]{1,2,0:T(8,128)} %get-tuple-element.8, f32[5,768]{1,0:T(8,128)S(1)} %copy-done.6, pred[768,2240]{0,1:T(8,128)(4,1)S(1)} %copy-done, bf16[192,5,128]{2,0,1:T(8,128)(2,1)S(1)} %copy.41, bf16[2048,5,128]{2,0,1:T(8,128)(2,1)} %copy.40), kind=kOutput, calls=%fused_computation.23 | convolution fusion | flops 2234040320 | bytes 39992320 | tf_op jit(solution)/shard_map/hqk,khd->qhd/dot_general | solution.py:32
  193.9 1.2 reshape.167
  195.1 2.3 copy.48
  197.4 0.0 all-to-all-done.4
  197.4 8.1 %all-to-all-start.3 = ((bf16[4,192,640]{2,1,0:T(8,128)(2,1)}), bf16[4,192,640]{2,1,0:T(8,128)(2,1)S(1)}, u32[]{:S(2)}, u32[]{:S(2)}) async-start(bf16[4,192,640]{2,1,0:T(8,128)(2,1)} %copy.48), calls=%async_computation.3 | async-start | bytes 1966080 | tf_op jit(solution)/shard_map/all_to_all | solution.py:80
  205.5 0.5 broadcast.104
  206.0 0.7 reduce.2
  206.8 0.1 reshape.175
  206.9 21.6 %all-to-all-done.3 = bf16[4,192,640]{2,1,0:T(8,128)(2,1)S(1)} async-done(((bf16[4,192,640]{2,1,0:T(8,128)(2,1)}), bf16[4,192,640]{2,1,0:T(8,128)(2,1)S(1)}, u32[]{:S(2)}, u32[]{:S(2)}) %all-to-all-start.3) | async-done | bytes 983072 | tf_op jit(solution)/shard_map/all_to_all | solution.py:80
  228.5 0.6 copy.49
  229.1 0.3 fusion.17
  229.4 0.1 divide_convert_fusion
  229.5 4.6 %convert_bitcast_fusion = bf16[8,192,640]{2,1,0:T(8,128)(2,1)S(1)} fusion(bf16[192,640,1]{0,1,2:T(8,128)(2,1)S(1)} %bitcast.46, bf16[80,8,8,640]{3,2,1,0:T(8,128)(2,1)} %bitcast.53), kind=kOutput, calls=%fused_computation.21 | convolution fusion | flops 1259274240 | bytes 8765440 | tf_op jit(solution)/shard_map/qf,fkc->kqc/dot_general | solution.py:92
  234.1 32.2 %all_to_all.31 = bf16[8,192,640]{2,1,0:T(8,128)(2,1)S(1)} all-to-all(bf16[8,192,640]{2,1,0:T(8,128)(2,1)S(1)} %convert_bitcast_fusion), channel_id=1, replica_groups=mesh['place'=4,'req'=8,'tp'=8] {'tp'}, dimensions={0} | all-to-all | bytes 3932160 | tf_op jit(solution)/shard_map/all_to_all | solution.py:95
  266.3 1.0 reduce_sum.45
  (24 shorter events, 0.1 us)
Async XLA Ops:
  23.7 14.0 %copy-start.7 = (s32[8]{0:T(128)S(1)}, s32[8]{0:T(128)}, u32[]{:S(2)}) copy-start(s32[8]{0:T(128)} %param.16) | copy-start | bytes 100
  23.7 14.6 %copy-start.8 = (s32[8]{0:T(128)S(1)}, s32[8]{0:T(128)}, u32[]{:S(2)}) copy-start(s32[8]{0:T(128)} %param.17) | copy-start | bytes 100
  23.7 15.2 %copy-start.9 = (s32[8]{0:T(128)S(1)}, s32[8]{0:T(128)}, u32[]{:S(2)}) copy-start(s32[8]{0:T(128)} %param.18) | copy-start | bytes 100
  23.7 15.8 %copy-start.2 = (bf16[192,640]{1,0:T(8,128)(2,1)S(1)}, bf16[192,640]{1,0:T(8,128)(2,1)}, u32[]{:S(2)}) copy-start(bf16[192,640]{1,0:T(8,128)(2,1)} %param.11) | copy-start | bytes 737284
  23.7 16.9 %copy-start.3 = (bf16[192,640]{1,0:T(8,128)(2,1)S(1)}, bf16[192,640]{1,0:T(8,128)(2,1)}, u32[]{:S(2)}) copy-start(bf16[192,640]{1,0:T(8,128)(2,1)} %param.12) | copy-start | bytes 737284
  23.7 70.9 %all-to-all-start.1 = ((bf16[8,256,640]{2,1,0:T(8,128)(2,1)}), bf16[8,256,640]{2,1,0:T(8,128)(2,1)S(1)}, u32[]{:S(2)}, u32[]{:S(2)}) async-start(bf16[8,256,640]{2,1,0:T(8,128)(2,1)} %param.13), calls=%async_computation.1 | async-start | bytes 5242880 | tf_op jit(solution)/shard_map/all_to_all | solution.py:61
  94.6 64.7 %all-to-all-start = ((bf16[8,256,640]{2,1,0:T(8,128)(2,1)}), bf16[8,256,640]{2,1,0:T(8,128)(2,1)}, u32[]{:S(2)}, u32[]{:S(2)}) async-start(bf16[8,256,640]{2,1,0:T(8,128)(2,1)} %param.14), calls=%async_computation | async-start | bytes 5242880 | tf_op jit(solution)/shard_map/all_to_all | solution.py:62
  113.8 2.7 %copy-start = (pred[768,2240]{0,1:T(8,128)(4,1)S(1)}, pred[768,2240]{0,1:T(8,128)(4,1)}, u32[]{:S(2)}) copy-start(pred[768,2240]{0,1:T(8,128)(4,1)} %fusion.7) | copy-start | bytes 5160964
  113.8 3.2 %copy-start.1 = (bf16[768,5,128]{2,1,0:T(8,128)(2,1)S(1)}, bf16[768,5,128]{2,1,0:T(8,128)(2,1)}, u32[]{:S(2)}) copy-start(bf16[768,5,128]{2,1,0:T(8,128)(2,1)} %reshape.173) | copy-start | bytes 2949124
  113.8 3.2 %copy-start.4 = (bf16[192,5,128]{2,0,1:T(8,128)(2,1)S(1)}, bf16[192,5,128]{2,0,1:T(8,128)(2,1)}, u32[]{:S(2)}) copy-start(bf16[192,5,128]{2,0,1:T(8,128)(2,1)} %copy.45) | copy-start | bytes 737284
  131.3 14.2 %copy-start.5 = (f32[5,768]{1,0:T(8,128)}, f32[5,768]{1,0:T(8,128)S(1)}, u32[]{:S(2)}) copy-start(f32[5,768]{1,0:T(8,128)S(1)} %get-tuple-element.7) | copy-start | bytes 46084
  159.3 38.1 %all-to-all-start.4 = ((f32[4,1,1920]{2,1,0:T(1,128)}), f32[4,1,1920]{2,1,0:T(1,128)S(1)}, u32[]{:S(2)}, u32[]{:S(2)}) async-start(f32[4,1,1920]{2,1,0:T(1,128)} %reshape.174), calls=%async_computation.4 | async-start | bytes 61440 | tf_op jit(solution)/shard_map/all_to_all | solution.py:84
  174.6 4.0 %copy-start.6 = (f32[5,768]{1,0:T(8,128)S(1)}, f32[5,768]{1,0:T(8,128)}, u32[]{:S(2)}) copy-start(f32[5,768]{1,0:T(8,128)} %copy-done.5) | copy-start | bytes 46084
  197.4 31.1 %all-to-all-start.3 = ((bf16[4,192,640]{2,1,0:T(8,128)(2,1)}), bf16[4,192,640]{2,1,0:T(8,128)(2,1)S(1)}, u32[]{:S(2)}, u32[]{:S(2)}) async-start(bf16[4,192,640]{2,1,0:T(8,128)(2,1)} %copy.48), calls=%async_computation.3 | async-start | bytes 1966080 | tf_op jit(solution)/shard_map/all_to_all | solution.py:80

commit v4 on v3

--- a/solution.py
+++ b/solution.py
@@ -51,37 +51,87 @@
     heads_here = width // HEAD
     places = lax.axis_size("place")
     group = lax.axis_size("req")
+    devices = places * group
     place = lax.axis_index("place")
     mine = lax.axis_index("req")
+    me = place * group + mine
     cache_dev = cache_keys.shape[1]
     length = cache_lengths[mine]
     window = windows[mine]
     sinks = sink_counts[mine]
+    seq = ("place", "req")
 
-    got_keys = lax.all_to_all(cache_keys, "req", split_axis=0, concat_axis=0, tiled=True)
-    got_vals = lax.all_to_all(cache_values, "req", split_axis=0, concat_axis=0, tiled=True)
-    span_q = lax.all_to_all(
-        jnp.broadcast_to(query[None], (places,) + query.shape), "place", split_axis=0, concat_axis=0, tiled=True
-    )
+    ring = devices // 4
+    core, z, y = me % 2, (me // 2) % ring, me // (2 * ring)
 
-    blocks = lax.dynamic_slice_in_dim(block_of_slot[mine], place * group, group)
+    def at(yy, zz, cc):
+        return (yy * ring + zz % ring) * 2 + cc
+
+    def request_of(index):
+        return index % group
+
+    moves = [(d, flip) for d in (-1, 0, 1) for flip in (0, 1)] + [("far", c) for c in (0, 1)]
+    got_keys, got_vals, got_slot = [], [], []
+    for d, flip in moves:
+        if d == "far":
+            target = jnp.where(core == 0, at(y, z + 2, flip), at(y, z - 2, 1 - flip))
+            source = jnp.where(core == flip, at(y, z - 2, 0), at(y, z + 2, 1))
+            pairs = []
+            for s_idx in range(devices):
+                sc, sz, sy = s_idx % 2, (s_idx // 2) % ring, s_idx // (2 * ring)
+                if sc == 0:
+                    pairs.append((s_idx, (sy * ring + (sz + 2) % ring) * 2 + flip))
+                else:
+                    pairs.append((s_idx, (sy * ring + (sz - 2) % ring) * 2 + 1 - flip))
+        else:
+            target = at(y, z + d, core ^ flip)
+            source = at(y, z - d, core ^ flip)
+            pairs = []
+            for s_idx in range(devices):
+                sc, sz, sy = s_idx % 2, (s_idx // 2) % ring, s_idx // (2 * ring)
+                pairs.append((s_idx, (sy * ring + (sz + d) % ring) * 2 + (sc ^ flip)))
+        sent = request_of(target)
+        chunk = (
+            lax.dynamic_index_in_dim(cache_keys, sent, 0, keepdims=False),
+            lax.dynamic_index_in_dim(cache_values, sent, 0, keepdims=False),
+        )
+        if d != 0 or flip != 0:
+            chunk = lax.ppermute(chunk, seq, pairs)
+        got_keys.append(chunk[0])
+        got_vals.append(chunk[1])
+        got_slot.append(source)
+
+    span_q = [query]
+    for k in range(1, places):
+        pairs = [(p * group + i, ((p + k) % places) * group + i) for p in range(places) for i in range(group)]
+        span_q.append(lax.ppermute(query, seq, pairs))
+    span_q = jnp.stack(span_q)
+    from_place = (place - jnp.arange(places, dtype=jnp.int32)) % places
+
+    slots = jnp.stack(got_slot)
+    blocks = block_of_slot[mine][slots]
     slot_pos = (blocks[:, None] * cache_dev + jnp.arange(cache_dev, dtype=jnp.int32)[None, :]).reshape(-1)
     own_pos = length + place * rows + jnp.arange(rows, dtype=jnp.int32)
-    query_pos = length + jnp.arange(places * rows, dtype=jnp.int32)
+    query_pos = (length + from_place[:, None] * rows + jnp.arange(rows, dtype=jnp.int32)[None, :]).reshape(-1)
 
-    keys = jnp.concatenate([got_keys.reshape(-1, width), span_keys], 0).reshape(-1, heads_here, HEAD)
-    vals = jnp.concatenate([got_vals.reshape(-1, width), span_values], 0).reshape(-1, heads_here, HEAD)
+    keys = jnp.concatenate(got_keys + [span_keys], 0).reshape(-1, heads_here, HEAD)
+    vals = jnp.concatenate(got_vals + [span_values], 0).reshape(-1, heads_here, HEAD)
     key_pos = jnp.concatenate([slot_pos, own_pos])
     valid = jnp.concatenate([slot_pos < length, jnp.ones((rows,), jnp.bool_)])
 
     summed, top, total = block_partial(
         span_q.reshape(-1, heads_here, HEAD), keys, vals, query_pos, key_pos, valid, window, sinks
     )
-    summed = lax.all_to_all(
-        summed.astype(jnp.bfloat16).reshape(places, rows, width), "place", split_axis=0, concat_axis=0, tiled=True
-    ).reshape(places, rows, heads_here, HEAD).astype(jnp.float32)
+    summed = summed.astype(jnp.bfloat16).reshape(places, rows, width)
     stats = jnp.concatenate([top, total], axis=1).reshape(places, rows, 2 * heads_here)
-    stats = lax.all_to_all(stats, "place", split_axis=0, concat_axis=0, tiled=True)
+    back_sum, back_stats = [summed[0]], [stats[0]]
+    for k in range(1, places):
+        pairs = [(p * group + i, ((p - k) % places) * group + i) for p in range(places) for i in range(group)]
+        got = lax.ppermute((summed[k], stats[k]), seq, pairs)
+        back_sum.append(got[0])
+        back_stats.append(got[1])
+    summed = jnp.stack(back_sum).astype(jnp.float32).reshape(places, rows, heads_here, HEAD)
+    stats = jnp.stack(back_stats)
     top, total = stats[..., :heads_here], stats[..., heads_here:]
     best = jnp.max(top, axis=0)
     factor = jnp.exp(top - best[None])

time: 270 us -> 256 us (0.948)
  waiting for transfers between devices: 85.9 us -> 39 us
  local copies, waits for them, and re-layouts: 31.7 us -> 62.8 us
  starting transfers between devices: 36.5 us -> 60.6 us
  blocking collectives: 54.9 us -> 33.6 us
    all_to_all x4 -> x0, waiting for transfers between devices: 85.9 us -> none  [the longest x1 51.4 us: shards(): lax.all_to_all(cache_keys, 'req', split_axis=0, concat_axis=0, tiled=True)]
    ppermute x0 -> x23, starting transfers between devices: none -> 60.6 us  [the longest x14 38.1 us: shards(): chunk = lax.ppermute(chunk, seq, pairs)]
    ppermute x0 -> x23, waiting for transfers between devices: none -> 39 us  [the longest x6 29 us: shards(): got = lax.ppermute((summed[k], stats[k]), seq, pairs)]
    all_to_all x4 -> x0, starting transfers between devices: 36.5 us -> none  [the longest x1 13.2 us: shards(): lax.all_to_all(cache_keys, 'req', split_axis=0, concat_axis=0, tiled=True)]
    all_to_all x1 -> x0, blocking collectives: 22.7 us -> none  [shards(): lax.all_to_all(jnp.broadcast_to(query[None], (places,) + query.shape), 'p...]
    dynamic_slice x0 -> x15, local copies, waits for them, and re-layouts: none -> 19 us  [the longest x8 11 us: shards(): lax.dynamic_index_in_dim(cache_keys, sent, 0, keepdims=False)]
    unnamed x25 -> x69, local copies, waits for them, and re-layouts: 1.68 us -> 12.5 us
    concatenate x6 -> x20, local copies, waits for them, and re-layouts: 19 us -> 26.3 us  [the longest x10 15 us: shards(): jnp.concatenate(got_keys + [span_keys], 0).reshape(-1, heads_here, HEAD)]
  transfers between devices with their start and end apart: 4 -> 23, of which waited for: 3 -> 7; matrix products, arithmetic and copies ran while one was open for 30% -> 22% of each run, Pallas kernels for 0% -> 0%
where the time goes in v4:
time: 256 us; the launch traced here: 255 us
  local copies, waits for them, and re-layouts  62.8 us (25%)
  starting transfers between devices  60.6 us (24%)
  waiting for transfers between devices  39 us (15%)
  matrix products  35.2 us (14%)
  blocking collectives  33.6 us (13%)
  other arithmetic  22.8 us (9%)
    ppermute x14, starting transfers between devices, shards(): chunk = lax.ppermute(chunk, seq, pairs)  38.1 us
    all_to_all x1, blocking collectives, shards(): lax.all_to_all(terms.astype(jnp.bfloat16), 'tp', split_axis=0, concat_axi...  33.6 us
    ppermute x6, waiting for transfers between devices, shards(): got = lax.ppermute((summed[k], stats[k]), seq, pairs)  29 us
    dot_general x1, matrix products, block_partial(): jnp.einsum('hqk,khd->qhd', weights.astype(jnp.bfloat16), vals, preferred_...  15.6 us
    dot_general x1, matrix products, block_partial(): jnp.einsum('qhd,khd->hqk', q_rows, keys, preferred_element_type=jnp.float32)  15.1 us
    ppermute x6, starting transfers between devices, shards(): got = lax.ppermute((summed[k], stats[k]), seq, pairs)  15 us
    concatenate x10, local copies, waits for them, and re-layouts, shards(): jnp.concatenate(got_keys + [span_keys], 0).reshape(-1, heads_here, HEAD)  15 us
    reduce_sum x1, other arithmetic, block_partial(): total = jnp.sum(weights, axis=2)  14.2 us
  transfers between devices with their start and end apart: 23, of which 7 were waited for; matrix products, arithmetic and copies ran while one was open for 22% of the time, Pallas kernels for 0%

profile of v4, /device:TPU:224, one launch (start us, length us, event | category | flops | bytes accessed | tf_op | source)
XLA Modules:
  0.0 255.2 jit_solution(3905699455965385860)
XLA Ops:
  0.0 2.5 collective-permute-start.7
  2.5 3.5 %collective-permute-start.9 = (bf16[192,640]{1,0:T(8,128)(2,1)}, bf16[192,640]{1,0:T(8,128)(2,1)}, u32[]{:S(2)}, u32[]{:S(2)}) collective-permute-start(bf16[192,640]{1,0:T(8,128)(2,1)} %param.10), channel_id=1, source_target_pairs={{0,192},{8,200},{16,208},{24,216},{32,224},{40,232},{48,240},{56,2... | collective-permute-start | bytes 737288 | tf_op jit(solution)/shard_map/ppermute | solution.py:107
  5.9 1.6 collective-permute-start.8
  7.5 4.1 %constant_dynamic-slice_fusion = (bf16[1,256,640]{2,1,0:T(8,128)(2,1)}, bf16[1,256,640]{2,1,0:T(8,128)(2,1)}, bf16[1,256,640]{2,1,0:T(8,128)(2,1)S(1)}, bf16[1,2...) fusion(bf16[8,256,640]{2,1,0:T(8,128)(2,1)} %param.13, ...), kind=kLoop, calls=%fused_computation.59 | loop fusion | bytes 10485792 | tf_op jit(solution)/shard_map/jit(dynamic_index_in_dim)/dynamic_slice | solution.py:95
  11.6 1.9 copy.19
  13.5 1.9 copy.17
  15.4 3.4 %collective-permute-start.4 = (bf16[256,640]{0,1:T(8,128)(2,1)}, bf16[256,640]{0,1:T(8,128)(2,1)}, u32[]{:S(2)}, u32[]{:S(2)}) collective-permute-start(bf16[256,640]{0,1:T(8,128)(2,1)} %bitcast.92), channel_id=1, source_target_pairs={{0,24},{8,16},{16,40},{24,32},{32,56},{40,48},{48,72},{56,64},{64,... | collective-permute-start | bytes 983048 | tf_op jit(solution)/shard_map/ppermute | solution.py:99
  20.8 1.9 copy.15
  22.7 1.9 copy.16
  25.7 1.8 collective-permute-done.9
  29.5 1.9 copy.38
  31.4 1.9 copy.36
  37.7 4.6 %collective-permute-start.1 = (bf16[256,640]{0,1:T(8,128)(2,1)S(1)}, bf16[256,640]{0,1:T(8,128)(2,1)S(1)}, u32[]{:S(2)}, u32[]{:S(2)}) collective-permute-start(bf16[256,640]{0,1:T(8,128)(2,1)S(1)} %bitcast.105), channel_id=1, source_target_pairs={{0,120},{8,112},{16,8},{24,0},{32,24},{40,16},{48,40},{56,32},{64,... | collective-permute-start | bytes 983048 | tf_op jit(solution)/shard_map/ppermute | solution.py:99
  42.4 1.4 collective-permute-start.5
  43.9 1.2 collective-permute-done.3
  45.0 4.0 %collective-permute-start.15 = (bf16[256,640]{0,1:T(8,128)(2,1)S(1)}, bf16[256,640]{0,1:T(8,128)(2,1)S(1)}, u32[]{:S(2)}, u32[]{:S(2)}) collective-permute-start(bf16[256,640]{0,1:T(8,128)(2,1)S(1)} %bitcast.101), channel_id=1, source_target_pairs={{0,32},{8,104},{16,48},{24,120},{32,64},{40,8},{48,80},{56,24},{64... | collective-permute-start | bytes 983048 | tf_op jit(solution)/shard_map/ppermute | solution.py:99
  50.4 2.2 collective-permute-start.11
  52.6 6.3 %collective-permute-done = bf16[256,640]{0,1:T(8,128)(2,1)S(1)} collective-permute-done((bf16[256,640]{0,1:T(8,128)(2,1)S(1)}, bf16[256,640]{0,1:T(8,128)(2,1)S(1)}, u32[]{:S(2)}, u32[]{:S(2)}) %collective-permute-start) | collective-permute-done | bytes 327712 | tf_op jit(solution)/shard_map/ppermute | solution.py:99
  59.2 16.4 %collective-permute-start.14 = (bf16[256,640]{0,1:T(8,128)(2,1)}, bf16[256,640]{0,1:T(8,128)(2,1)}, u32[]{:S(2)}, u32[]{:S(2)}) collective-permute-start(bf16[256,640]{0,1:T(8,128)(2,1)} %bitcast.42), channel_id=1, source_target_pairs={{0,24},{8,16},{16,40},{24,32},{32,56},{40,48},{48,72},{56,64},{64,... | collective-permute-start | bytes 983048 | tf_op jit(solution)/shard_map/ppermute | solution.py:99
  75.6 4.5 %collective-permute-start.16 = (bf16[256,640]{0,1:T(8,128)(2,1)}, bf16[256,640]{0,1:T(8,128)(2,1)}, u32[]{:S(2)}, u32[]{:S(2)}) collective-permute-start(bf16[256,640]{0,1:T(8,128)(2,1)} %bitcast.46), channel_id=1, source_target_pairs={{0,40},{8,96},{16,56},{24,112},{32,72},{40,0},{48,88},{56,16},{64,... | collective-permute-start | bytes 983048 | tf_op jit(solution)/shard_map/ppermute | solution.py:99
  80.2 3.6 %fusion.7 = pred[768,2240]{0,1:T(8,128)(4,1)S(1)} fusion(s32[]{:T(128)} %bitcast.27, s32[768]{0:T(1024)S(1)} %add.320, s32[2240]{0:T(1024)S(1)} %pad_add_fusion, pred[2240]{0:T(1024)(128)(4,1)S(1)} %concatenate.88, pred[2240]{0:T(1024)(128)(4,1)S(1)} %broadcast_compare_fusion), kind=kLoop, calls=%fused_computation.10 | loop fusion | flops 10321920 | bytes 1736836 | tf_op jit(solution)/shard_map/and | solution.py:21
  87.3 1.5 pad_maximum_fusion
  88.8 2.1 reshape.539
  90.8 1.2 copy.28
  92.1 1.2 copy.26
  93.3 1.2 copy.25
  94.4 1.9 copy.24
  96.3 1.9 copy.22
  99.1 1.2 copy.27
  100.3 1.9 copy.46
  102.2 1.9 copy.40
  104.1 1.9 copy.41
  106.0 1.9 copy.43
  107.9 1.9 copy.44
  109.7 1.9 copy.45
  111.6 1.9 copy.47
  113.5 1.1 constant_dynamic-update-slice_fusion.17
  114.6 1.8 constant_dynamic-update-slice_fusion.8
  126.3 15.1 %fusion.31 = (f32[5,768]{1,0:T(8,128)S(1)}, f32[5,768,2240]{1,2,0:T(8,128)}) fusion(bf16[2240,5,128]{2,0,1:T(8,128)(2,1)} %copy-done.20, bf16[768,5,128]{2,1,0:T(8,128)(2,1)S(1)} %copy-done.2, pred[768,2240]{0,1:T(8,128)(4,1)S(1)} %fusion.7), kind=kOutput, calls=%fused_computation.91 | convolution fusion | flops 2227810560 | bytes 39992320 | tf_op jit(solution)/shard_map/qhd,khd->hqk/dot_general | solution.py:27
  141.3 14.2 %fusion = f32[5,768]{1,0:T(8,128)S(1)} fusion(f32[5,768,2240]{1,2,0:T(8,128)} %get-tuple-element.32, f32[5,768]{1,0:T(8,128)S(1)} %get-tuple-element.31, pred[768,2240]{0,1:T(8,128)(4,1)S(1)} %fusion.7), kind=kLoop, calls=%fused_computation.3 | loop fusion | flops 25800960 | bytes 36157440 | tf_op jit(solution)/shard_map/reduce_sum | solution.py:31
  155.5 15.6 %fusion.16 = bf16[768,5,128]{0,2,1:T(8,128)(2,1)S(1)} fusion(bf16[2240,5,128]{2,0,1:T(8,128)(2,1)} %constant_dynamic-update-slice_fusion, f32[5,768,2240]{1,2,0:T(8,128)} %get-tuple-element.32, f32[5,768]{1,0:T(8,128)S(1)} %get-tuple-element.31, pred[768,2240]{0,1:T(8,128)(4,1)S(1)} %fusion.7), kind=kOutput, calls=%fused_computation.17 | convolution fusion | flops 2228305920 | bytes 39992320 | tf_op jit(solution)/shard_map/hqk,khd->qhd/dot_general | solution.py:32
  171.1 6.9 %collective-permute-start.20 = (f32[192,10]{0,1:T(8,128)S(1)}, f32[192,10]{0,1:T(8,128)S(1)}, u32[]{:S(2)}, u32[]{:S(2)}) collective-permute-start(f32[192,10]{0,1:T(8,128)S(1)} %get-tuple-element.28), channel_id=1, source_target_pairs={{0,192},{8,200},{16,208},{24,216},{32,224},{40,232},{48,240},{56,2... | collective-permute-start | bytes 23048 | tf_op jit(solution)/shard_map/ppermute | solution.py:130
  178.1 1.9 collective-permute-start.21
  180.2 5.6 %collective-permute-start.19 = (bf16[192,640]{0,1:T(8,128)(2,1)S(1)}, bf16[192,640]{0,1:T(8,128)(2,1)S(1)}, u32[]{:S(2)}, u32[]{:S(2)}) collective-permute-start(bf16[192,640]{0,1:T(8,128)(2,1)S(1)} %bitcast.91), channel_id=1, source_target_pairs={{0,64},{8,72},{16,80},{24,88},{32,96},{40,104},{48,112},{56,120},{... | collective-permute-start | bytes 737288 | tf_op jit(solution)/shard_map/ppermute | solution.py:130
  186.6 14.7 %collective-permute-done.19 = bf16[192,640]{0,1:T(8,128)(2,1)S(1)} collective-permute-done((bf16[192,640]{0,1:T(8,128)(2,1)S(1)}, bf16[192,640]{0,1:T(8,128)(2,1)S(1)}, u32[]{:S(2)}, u32[]{:S(2)}) %collective-permute-start.19) | collective-permute-done | bytes 245792 | tf_op jit(solution)/shard_map/ppermute | solution.py:130
  201.3 14.3 %collective-permute-done.17 = bf16[192,640]{0,1:T(8,128)(2,1)S(1)} collective-permute-done((bf16[192,640]{0,1:T(8,128)(2,1)S(1)}, bf16[192,640]{0,1:T(8,128)(2,1)S(1)}, u32[]{:S(2)}, u32[]{:S(2)}) %collective-permute-start.17) | collective-permute-done | bytes 245792 | tf_op jit(solution)/shard_map/ppermute | solution.py:130
  216.0 4.6 %convert_bitcast_fusion = bf16[8,192,640]{2,1,0:T(8,128)(2,1)S(1)} fusion(bf16[192,640,1]{0,1,2:T(8,128)(2,1)S(1)} %bitcast.106, bf16[80,8,8,640]{3,2,1,0:T(8,128)(2,1)} %bitcast.120), kind=kOutput, calls=%fused_computation.15 | convolution fusion | flops 1259274240 | bytes 8765440 | tf_op jit(solution)/shard_map/qf,fkc->kqc/dot_general | solution.py:142
  220.6 33.6 %all_to_all.5 = bf16[8,192,640]{2,1,0:T(8,128)(2,1)S(1)} all-to-all(bf16[8,192,640]{2,1,0:T(8,128)(2,1)S(1)} %convert_bitcast_fusion), channel_id=1, replica_groups=mesh['place'=4,'req'=8,'tp'=8] {'tp'}, dimensions={0} | all-to-all | bytes 3932160 | tf_op jit(solution)/shard_map/all_to_all | solution.py:145
  (136 shorter events, 27.3 us)
Async XLA Ops:
  0.0 19.5 %copy-start = (s32[8,32]{1,0:T(8,128)S(1)}, s32[8,32]{1,0:T(8,128)}, u32[]{:S(2)}) copy-start(s32[8,32]{1,0:T(8,128)} %param.19) | copy-start | bytes 3076
  0.0 24.6 %collective-permute-start.7 = (bf16[192,640]{1,0:T(8,128)(2,1)}, bf16[192,640]{1,0:T(8,128)(2,1)S(1)}, u32[]{:S(2)}, u32[]{:S(2)}) collective-permute-start(bf16[192,640]{1,0:T(8,128)(2,1)} %param.10), channel_id=1, source_target_pairs={{0,64},{8,72},{16,80},{24,88},{32,96},{40,104},{48,112},{56,120},{... | collective-permute-start | bytes 737288 | tf_op jit(solution)/shard_map/ppermute | solution.py:107
  2.5 25.0 %collective-permute-start.9 = (bf16[192,640]{1,0:T(8,128)(2,1)}, bf16[192,640]{1,0:T(8,128)(2,1)}, u32[]{:S(2)}, u32[]{:S(2)}) collective-permute-start(bf16[192,640]{1,0:T(8,128)(2,1)} %param.10), channel_id=1, source_target_pairs={{0,192},{8,200},{16,208},{24,216},{32,224},{40,232},{48,240},{56,2... | collective-permute-start | bytes 737288 | tf_op jit(solution)/shard_map/ppermute | solution.py:107
  5.9 31.7 %collective-permute-start.8 = (bf16[192,640]{1,0:T(8,128)(2,1)}, bf16[192,640]{1,0:T(8,128)(2,1)}, u32[]{:S(2)}, u32[]{:S(2)}) collective-permute-start(bf16[192,640]{1,0:T(8,128)(2,1)} %param.10), channel_id=1, source_target_pairs={{0,128},{8,136},{16,144},{24,152},{32,160},{40,168},{48,176},{56,1... | collective-permute-start | bytes 737288 | tf_op jit(solution)/shard_map/ppermute | solution.py:107
  7.5 11.4 %copy-start.21 = (s32[8]{0:T(128)S(1)}, s32[8]{0:T(128)}, u32[]{:S(2)}) copy-start(s32[8]{0:T(128)} %param.16) | copy-start | bytes 100
  11.6 15.9 %copy-start.22 = (s32[8]{0:T(128)S(1)}, s32[8]{0:T(128)}, u32[]{:S(2)}) copy-start(s32[8]{0:T(128)} %param.18) | copy-start | bytes 100
  11.6 16.5 %copy-start.23 = (s32[8]{0:T(128)S(1)}, s32[8]{0:T(128)}, u32[]{:S(2)}) copy-start(s32[8]{0:T(128)} %param.17) | copy-start | bytes 100
  13.5 28.8 %collective-permute-start.6 = (bf16[256,640]{0,1:T(8,128)(2,1)}, bf16[256,640]{0,1:T(8,128)(2,1)}, u32[]{:S(2)}, u32[]{:S(2)}) collective-permute-start(bf16[256,640]{0,1:T(8,128)(2,1)} %bitcast.93), channel_id=1, source_target_pairs={{0,40},{8,96},{16,56},{24,112},{32,72},{40,0},{48,88},{56,16},{64,... | collective-permute-start | bytes 983048 | tf_op jit(solution)/shard_map/ppermute | solution.py:99
  15.4 27.0 %collective-permute-start.4 = (bf16[256,640]{0,1:T(8,128)(2,1)}, bf16[256,640]{0,1:T(8,128)(2,1)}, u32[]{:S(2)}, u32[]{:S(2)}) collective-permute-start(bf16[256,640]{0,1:T(8,128)(2,1)} %bitcast.92), channel_id=1, source_target_pairs={{0,24},{8,16},{16,40},{24,32},{32,56},{40,48},{48,72},{56,64},{64,... | collective-permute-start | bytes 983048 | tf_op jit(solution)/shard_map/ppermute | solution.py:99
  24.6 12.2 %copy-start.19 = (bf16[192,640]{1,0:T(8,128)(2,1)}, bf16[192,640]{1,0:T(8,128)(2,1)S(1)}, u32[]{:S(2)}) copy-start(bf16[192,640]{1,0:T(8,128)(2,1)S(1)} %collective-permute-done.7) | copy-start | bytes 737284
  24.6 20.4 %collective-permute-start.3 = (bf16[256,640]{0,1:T(8,128)(2,1)}, bf16[256,640]{0,1:T(8,128)(2,1)}, u32[]{:S(2)}, u32[]{:S(2)}) collective-permute-start(bf16[256,640]{0,1:T(8,128)(2,1)} %bitcast.102), channel_id=1, source_target_pairs={{0,16},{8,24},{16,32},{24,40},{32,48},{40,56},{48,64},{56,72},{64,... | collective-permute-start | bytes 983048 | tf_op jit(solution)/shard_map/ppermute | solution.py:99
  27.5 21.5 %collective-permute-start.2 = (bf16[256,640]{0,1:T(8,128)(2,1)}, bf16[256,640]{0,1:T(8,128)(2,1)}, u32[]{:S(2)}, u32[]{:S(2)}) collective-permute-start(bf16[256,640]{0,1:T(8,128)(2,1)} %bitcast.100), channel_id=1, source_target_pairs={{0,8},{8,0},{16,24},{24,16},{32,40},{40,32},{48,56},{56,48},{64,72... | collective-permute-start | bytes 983048 | tf_op jit(solution)/shard_map/ppermute | solution.py:99
  35.1 48.6 %copy-start.17 = (bf16[192,640]{1,0:T(8,128)(2,1)S(1)}, bf16[192,640]{1,0:T(8,128)(2,1)}, u32[]{:S(2)}) copy-start(bf16[192,640]{1,0:T(8,128)(2,1)} %param.11) | copy-start | bytes 737284
  36.2 48.6 %copy-start.18 = (bf16[192,640]{1,0:T(8,128)(2,1)S(1)}, bf16[192,640]{1,0:T(8,128)(2,1)}, u32[]{:S(2)}) copy-start(bf16[192,640]{1,0:T(8,128)(2,1)} %param.12) | copy-start | bytes 737284
  37.7 12.7 %collective-permute-start.1 = (bf16[256,640]{0,1:T(8,128)(2,1)S(1)}, bf16[256,640]{0,1:T(8,128)(2,1)S(1)}, u32[]{:S(2)}, u32[]{:S(2)}) collective-permute-start(bf16[256,640]{0,1:T(8,128)(2,1)S(1)} %bitcast.105), channel_id=1, source_target_pairs={{0,120},{8,112},{16,8},{24,0},{32,24},{40,16},{48,40},{56,32},{64,... | collective-permute-start | bytes 983048 | tf_op jit(solution)/shard_map/ppermute | solution.py:99
  42.3 16.6 %collective-permute-start = (bf16[256,640]{0,1:T(8,128)(2,1)S(1)}, bf16[256,640]{0,1:T(8,128)(2,1)S(1)}, u32[]{:S(2)}, u32[]{:S(2)}) collective-permute-start(bf16[256,640]{0,1:T(8,128)(2,1)S(1)} %bitcast.104), channel_id=1, source_target_pairs={{0,112},{8,120},{16,0},{24,8},{32,16},{40,24},{48,32},{56,40},{64,... | collective-permute-start | bytes 983048 | tf_op jit(solution)/shard_map/ppermute | solution.py:99
  42.4 16.5 %collective-permute-start.5 = (bf16[256,640]{0,1:T(8,128)(2,1)S(1)}, bf16[256,640]{0,1:T(8,128)(2,1)S(1)}, u32[]{:S(2)}, u32[]{:S(2)}) collective-permute-start(bf16[256,640]{0,1:T(8,128)(2,1)S(1)} %bitcast.103), channel_id=1, source_target_pairs={{0,32},{8,104},{16,48},{24,120},{32,64},{40,8},{48,80},{56,24},{64... | collective-permute-start | bytes 983048 | tf_op jit(solution)/shard_map/ppermute | solution.py:99
  45.0 14.2 %collective-permute-start.15 = (bf16[256,640]{0,1:T(8,128)(2,1)S(1)}, bf16[256,640]{0,1:T(8,128)(2,1)S(1)}, u32[]{:S(2)}, u32[]{:S(2)}) collective-permute-start(bf16[256,640]{0,1:T(8,128)(2,1)S(1)} %bitcast.101), channel_id=1, source_target_pairs={{0,32},{8,104},{16,48},{24,120},{32,64},{40,8},{48,80},{56,24},{64... | collective-permute-start | bytes 983048 | tf_op jit(solution)/shard_map/ppermute | solution.py:99
  49.0 26.6 %collective-permute-start.10 = (bf16[256,640]{0,1:T(8,128)(2,1)S(1)}, bf16[256,640]{0,1:T(8,128)(2,1)S(1)}, u32[]{:S(2)}, u32[]{:S(2)}) collective-permute-start(bf16[256,640]{0,1:T(8,128)(2,1)S(1)} %bitcast.98), channel_id=1, source_target_pairs={{0,112},{8,120},{16,0},{24,8},{32,16},{40,24},{48,32},{56,40},{64,... | collective-permute-start | bytes 983048 | tf_op jit(solution)/shard_map/ppermute | solution.py:99
  50.4 29.8 %copy-start.11 = (bf16[256,640]{0,1:T(8,128)(2,1)}, bf16[256,640]{0,1:T(8,128)(2,1)S(1)}, u32[]{:S(2)}) copy-start(bf16[256,640]{0,1:T(8,128)(2,1)S(1)} %collective-permute-done.1) | copy-start | bytes 983044
  50.4 53.7 %collective-permute-start.11 = (bf16[256,640]{0,1:T(8,128)(2,1)}, bf16[256,640]{0,1:T(8,128)(2,1)}, u32[]{:S(2)}, u32[]{:S(2)}) collective-permute-start(bf16[256,640]{0,1:T(8,128)(2,1)} %bitcast.35), channel_id=1, source_target_pairs={{0,120},{8,112},{16,8},{24,0},{32,24},{40,16},{48,40},{56,32},{64,... | collective-permute-start | bytes 983048 | tf_op jit(solution)/shard_map/ppermute | solution.py:99
  58.9 21.3 %copy-start.12 = (bf16[256,640]{0,1:T(8,128)(2,1)}, bf16[256,640]{0,1:T(8,128)(2,1)S(1)}, u32[]{:S(2)}) copy-start(bf16[256,640]{0,1:T(8,128)(2,1)S(1)} %collective-permute-done) | copy-start | bytes 983044
  58.9 47.1 %collective-permute-start.12 = (bf16[256,640]{0,1:T(8,128)(2,1)}, bf16[256,640]{0,1:T(8,128)(2,1)}, u32[]{:S(2)}, u32[]{:S(2)}) collective-permute-start(bf16[256,640]{0,1:T(8,128)(2,1)} %bitcast.38), channel_id=1, source_target_pairs={{0,8},{8,0},{16,24},{24,16},{32,40},{40,32},{48,56},{56,48},{64,72... | collective-permute-start | bytes 983048 | tf_op jit(solution)/shard_map/ppermute | solution.py:99
  58.9 21.3 %copy-start.14 = (bf16[256,640]{0,1:T(8,128)(2,1)}, bf16[256,640]{0,1:T(8,128)(2,1)S(1)}, u32[]{:S(2)}) copy-start(bf16[256,640]{0,1:T(8,128)(2,1)S(1)} %collective-permute-done.5) | copy-start | bytes 983044
  58.9 48.9 %collective-permute-start.13 = (bf16[256,640]{0,1:T(8,128)(2,1)}, bf16[256,640]{0,1:T(8,128)(2,1)}, u32[]{:S(2)}, u32[]{:S(2)}) collective-permute-start(bf16[256,640]{0,1:T(8,128)(2,1)} %bitcast.40), channel_id=1, source_target_pairs={{0,16},{8,24},{16,32},{24,40},{32,48},{40,56},{48,64},{56,72},{64,... | collective-permute-start | bytes 983048 | tf_op jit(solution)/shard_map/ppermute | solution.py:99
  59.2 21.0 %copy-start.15 = (bf16[256,640]{0,1:T(8,128)(2,1)}, bf16[256,640]{0,1:T(8,128)(2,1)S(1)}, u32[]{:S(2)}) copy-start(bf16[256,640]{0,1:T(8,128)(2,1)S(1)} %collective-permute-done.15) | copy-start | bytes 983044
  59.2 50.5 %collective-permute-start.14 = (bf16[256,640]{0,1:T(8,128)(2,1)}, bf16[256,640]{0,1:T(8,128)(2,1)}, u32[]{:S(2)}, u32[]{:S(2)}) collective-permute-start(bf16[256,640]{0,1:T(8,128)(2,1)} %bitcast.42), channel_id=1, source_target_pairs={{0,24},{8,16},{16,40},{24,32},{32,56},{40,48},{48,72},{56,64},{64,... | collective-permute-start | bytes 983048 | tf_op jit(solution)/shard_map/ppermute | solution.py:99
  75.6 4.6 %copy-start.16 = (bf16[256,640]{0,1:T(8,128)(2,1)}, bf16[256,640]{0,1:T(8,128)(2,1)S(1)}, u32[]{:S(2)}) copy-start(bf16[256,640]{0,1:T(8,128)(2,1)S(1)} %collective-permute-done.10) | copy-start | bytes 983044
  75.6 36.0 %collective-permute-start.16 = (bf16[256,640]{0,1:T(8,128)(2,1)}, bf16[256,640]{0,1:T(8,128)(2,1)}, u32[]{:S(2)}, u32[]{:S(2)}) collective-permute-start(bf16[256,640]{0,1:T(8,128)(2,1)} %bitcast.46), channel_id=1, source_target_pairs={{0,40},{8,96},{16,56},{24,112},{32,72},{40,0},{48,88},{56,16},{64,... | collective-permute-start | bytes 983048 | tf_op jit(solution)/shard_map/ppermute | solution.py:99
  90.8 7.4 %copy-start.13 = (bf16[256,640]{0,1:T(8,128)(2,1)S(1)}, bf16[256,640]{0,1:T(8,128)(2,1)}, u32[]{:S(2)}) copy-start(bf16[256,640]{0,1:T(8,128)(2,1)} %copy-done.12) | copy-start | bytes 983044
  113.5 6.1 %copy-start.6 = (bf16[256,5,128]{2,0,1:T(8,128)(2,1)S(1)}, bf16[256,5,128]{2,0,1:T(8,128)(2,1)}, u32[]{:S(2)}) copy-start(bf16[256,5,128]{2,0,1:T(8,128)(2,1)} %copy.44) | copy-start | bytes 983044
  113.5 6.1 %copy-start.7 = (bf16[256,5,128]{2,0,1:T(8,128)(2,1)S(1)}, bf16[256,5,128]{2,0,1:T(8,128)(2,1)}, u32[]{:S(2)}) copy-start(bf16[256,5,128]{2,0,1:T(8,128)(2,1)} %copy.45) | copy-start | bytes 983044
  113.5 6.2 %copy-start.5 = (bf16[256,5,128]{2,0,1:T(8,128)(2,1)S(1)}, bf16[256,5,128]{2,0,1:T(8,128)(2,1)}, u32[]{:S(2)}) copy-start(bf16[256,5,128]{2,0,1:T(8,128)(2,1)} %copy.46) | copy-start | bytes 983044
  113.5 6.3 %copy-start.8 = (bf16[256,5,128]{2,0,1:T(8,128)(2,1)S(1)}, bf16[256,5,128]{2,0,1:T(8,128)(2,1)}, u32[]{:S(2)}) copy-start(bf16[256,5,128]{2,0,1:T(8,128)(2,1)} %copy.47) | copy-start | bytes 983044
  113.5 6.3 %copy-start.10 = (bf16[192,5,128]{2,0,1:T(8,128)(2,1)S(1)}, bf16[192,5,128]{2,0,1:T(8,128)(2,1)}, u32[]{:S(2)}) copy-start(bf16[192,5,128]{2,0,1:T(8,128)(2,1)} %copy.48) | copy-start | bytes 737284
  114.6 5.3 %copy-start.4 = (bf16[256,5,128]{2,0,1:T(8,128)(2,1)S(1)}, bf16[256,5,128]{2,0,1:T(8,128)(2,1)}, u32[]{:S(2)}) copy-start(bf16[256,5,128]{2,0,1:T(8,128)(2,1)} %copy.22) | copy-start | bytes 983044
  117.5 4.0 %copy-start.3 = (bf16[256,5,128]{2,0,1:T(8,128)(2,1)S(1)}, bf16[256,5,128]{2,0,1:T(8,128)(2,1)}, u32[]{:S(2)}) copy-start(bf16[256,5,128]{2,0,1:T(8,128)(2,1)} %copy.24) | copy-start | bytes 983044
  119.8 5.7 %copy-start.9 = (bf16[192,5,128]{2,0,1:T(8,128)(2,1)S(1)}, bf16[192,5,128]{2,0,1:T(8,128)(2,1)}, u32[]{:S(2)}) copy-start(bf16[192,5,128]{2,0,1:T(8,128)(2,1)} %copy.29) | copy-start | bytes 737284
  119.9 6.4 %copy-start.2 = (bf16[768,5,128]{2,1,0:T(8,128)(2,1)S(1)}, bf16[768,5,128]{2,1,0:T(8,128)(2,1)}, u32[]{:S(2)}) copy-start(bf16[768,5,128]{2,1,0:T(8,128)(2,1)} %reshape.539) | copy-start | bytes 2949124
  119.9 5.5 %copy-start.20 = (bf16[2240,5,128]{2,0,1:T(8,128)(2,1)}, bf16[2240,5,128]{2,0,1:T(8,128)(2,1)S(1)}, u32[]{:S(2)}) copy-start(bf16[2240,5,128]{2,0,1:T(8,128)(2,1)S(1)} %constant_dynamic-update-slice_fusion.9) | copy-start | bytes 8601604
  171.1 14.9 %collective-permute-start.20 = (f32[192,10]{0,1:T(8,128)S(1)}, f32[192,10]{0,1:T(8,128)S(1)}, u32[]{:S(2)}, u32[]{:S(2)}) collective-permute-start(f32[192,10]{0,1:T(8,128)S(1)} %get-tuple-element.28), channel_id=1, source_target_pairs={{0,192},{8,200},{16,208},{24,216},{32,224},{40,232},{48,240},{56,2... | collective-permute-start | bytes 23048 | tf_op jit(solution)/shard_map/ppermute | solution.py:130
  178.1 8.5 %collective-permute-start.22 = (f32[192,10]{0,1:T(8,128)S(1)}, f32[192,10]{0,1:T(8,128)S(1)}, u32[]{:S(2)}, u32[]{:S(2)}) collective-permute-start(f32[192,10]{0,1:T(8,128)S(1)} %get-tuple-element.29), channel_id=1, source_target_pairs={{0,64},{8,72},{16,80},{24,88},{32,96},{40,104},{48,112},{56,120},{... | collective-permute-start | bytes 23048 | tf_op jit(solution)/shard_map/ppermute | solution.py:130
  178.1 8.5 %collective-permute-start.21 = (f32[192,10]{0,1:T(8,128)S(1)}, f32[192,10]{0,1:T(8,128)S(1)}, u32[]{:S(2)}, u32[]{:S(2)}) collective-permute-start(f32[192,10]{0,1:T(8,128)S(1)} %get-tuple-element.30), channel_id=1, source_target_pairs={{0,128},{8,136},{16,144},{24,152},{32,160},{40,168},{48,176},{56,1... | collective-permute-start | bytes 23048 | tf_op jit(solution)/shard_map/ppermute | solution.py:130
  180.2 21.0 %collective-permute-start.19 = (bf16[192,640]{0,1:T(8,128)(2,1)S(1)}, bf16[192,640]{0,1:T(8,128)(2,1)S(1)}, u32[]{:S(2)}, u32[]{:S(2)}) collective-permute-start(bf16[192,640]{0,1:T(8,128)(2,1)S(1)} %bitcast.91), channel_id=1, source_target_pairs={{0,64},{8,72},{16,80},{24,88},{32,96},{40,104},{48,112},{56,120},{... | collective-permute-start | bytes 737288 | tf_op jit(solution)/shard_map/ppermute | solution.py:130
  185.8 15.4 %collective-permute-start.18 = (bf16[192,640]{0,1:T(8,128)(2,1)S(1)}, bf16[192,640]{0,1:T(8,128)(2,1)S(1)}, u32[]{:S(2)}, u32[]{:S(2)}) collective-permute-start(bf16[192,640]{0,1:T(8,128)(2,1)S(1)} %bitcast.90), channel_id=1, source_target_pairs={{0,128},{8,136},{16,144},{24,152},{32,160},{40,168},{48,176},{56,1... | collective-permute-start | bytes 737288 | tf_op jit(solution)/shard_map/ppermute | solution.py:130
  186.0 29.5 %collective-permute-start.17 = (bf16[192,640]{0,1:T(8,128)(2,1)S(1)}, bf16[192,640]{0,1:T(8,128)(2,1)S(1)}, u32[]{:S(2)}, u32[]{:S(2)}) collective-permute-start(bf16[192,640]{0,1:T(8,128)(2,1)S(1)} %bitcast.89), channel_id=1, source_target_pairs={{0,192},{8,200},{16,208},{24,216},{32,224},{40,232},{48,240},{56,2... | collective-permute-start | bytes 737288 | tf_op jit(solution)/shard_map/ppermute | solution.py:130
  216.0 39.2 %copy-start.1 = (s32[8,32]{1,0:T(8,128)S(1)}, s32[8,32]{1,0:T(8,128)}, u32[]{:S(2)}) copy-start(s32[8,32]{1,0:T(8,128)} %param.19) | copy-start | bytes 3076
